TPU v7x, 512 devices: a whole 4x4x16 slice. The times are simulated.
512 devices in a mesh: ra: 64 (over z_lo, x, core), dec: 8 (over y, z_hi).
Axes of the slice: x: 4, y: 4, z: 16 (z_hi: 2, z_lo: 8; z = z_hi * 8 + z_lo), core: 2. Of those that a mesh axis runs over, the one named last changes fastest.
Arguments:
- exposure: float32 [131072, 2048], P(('ra', 'dec')), may hold values from -6 to 6
- slots: int32 [131072, 1], P(('ra', 'dec')), may hold values from 0 to 4; in each aligned block of 256 rows (0 to 255, 256 to 511, ...) at most 128 rows name the same one
- target_rows: int32 [131072], P(('ra', 'dec')), may hold values from 0 to 63
- template: bfloat16 [512, 131072], P('dec', 'ra'), may hold values from -6 to 6
- row_taps: bfloat16 [45, 21], replicated, may hold values from -1.25 to 1.25
- col_taps: bfloat16 [45, 21], replicated, may hold values from -1.25 to 1.25
- coef: float32 [45, 6], replicated, may hold values from -0.6 to 0.6
Outputs:
- difference: float32 [512, 131072], P('dec', 'ra')
Inputs may be any that keep to these rules, and one draw needn't show every extreme that they name: `slots`: among the rows of one device no value is taken by more than 128 rows; on some devices some value is taken by exactly 128.
All inputs are finite; a program needn't handle non-finite values.
Results may differ from a plain program's by a relative error of at most 0.0017.
Values may be sent and summed in bfloat16 or wider, within the bound.
A program may use at most 64 MiB of HBM per device.

v0:
```python
import math

import jax
import jax.numpy as jnp
from jax import lax
from jax.sharding import PartitionSpec as P

SPAN = 2
HALF = 10


def shifted(value, axis, by):
    length = lax.axis_size(axis)
    return lax.ppermute(value, axis, [(i, (i + by) % length) for i in range(length)])


def extended(value, sides, width, wrap):
    for axis, dim in sides:
        size, length = (lax.axis_size(axis), value.shape[dim])
        up = [(i, (i + 1) % size) for i in range(size if wrap else size - 1)]
        down = [(j, i) for i, j in up]
        last = lax.slice_in_dim(value, length - width, length, axis=dim)
        initial = lax.slice_in_dim(value, 0, width, axis=dim)
        before = lax.ppermute(last, axis, up)
        after = lax.ppermute(initial, axis, down)
        value = jnp.concatenate([before, value, after], axis=dim)
    return value


def band_table(taps, inner, outer):
    count = taps.shape[1]
    offset = (
        jnp.arange(inner, dtype=jnp.int32)[:, None] - jnp.arange(outer, dtype=jnp.int32)[None, :]
    )
    picks = (offset[None, :, :] == jnp.arange(count, dtype=jnp.int32)[:, None, None]).astype(
        jnp.float32
    )
    return jnp.einsum("kq,qab->kab", taps.astype(jnp.float32), picks).astype(jnp.bfloat16)


def local(exposure, slots, target_rows, template, row_taps, col_taps, coef):
    e_rows, width = exposure.shape
    p_rows = template.shape[0]
    n_slots = 2 * SPAN + 1
    capacity = e_rows // 2
    slot_ids = slots[:, 0]
    onehot = (slot_ids[:, None] == jnp.arange(n_slots, dtype=jnp.int32)[None, :]).astype(jnp.int32)
    position = jnp.sum((jnp.cumsum(onehot, axis=0) - onehot) * onehot, axis=1)
    flat_place = slot_ids * capacity + position
    select_int = (
        jnp.arange(n_slots * capacity, dtype=jnp.int32)[:, None] == flat_place[None, :]
    ).astype(jnp.int32)
    occupied = jnp.sum(select_int, axis=1)
    flat_rows = jnp.sum(select_int * target_rows[None, :], axis=1) + (1 - occupied) * p_rows
    outgoing = jnp.dot(
        select_int.astype(jnp.float32),
        exposure,
        precision=lax.Precision.HIGHEST,
        preferred_element_type=jnp.float32,
    ).reshape(n_slots, capacity, width)
    out_rows = flat_rows.reshape(n_slots, capacity)
    arrived = [outgoing[SPAN]]
    arrived_rows = [out_rows[SPAN]]
    for offset in range(-SPAN, SPAN + 1):
        if offset != 0:
            got_data, got_rows = shifted(
                (outgoing[SPAN + offset], out_rows[SPAN + offset]), "ra", offset
            )
            arrived.append(got_data)
            arrived_rows.append(got_rows)
    widened = extended(template, (("ra", 1),), HALF, True)
    all_rows = jnp.concatenate(arrived_rows)
    placing = (jnp.arange(p_rows, dtype=jnp.int32)[:, None] == all_rows[None, :]).astype(
        jnp.float32
    )
    science = jnp.dot(
        placing,
        jnp.concatenate(arrived, axis=0),
        precision=lax.Precision.HIGHEST,
        preferred_element_type=jnp.float32,
    )
    padded = extended(widened, (("dec", 0),), HALF, False)
    tile_cols = min(128, width)
    n_tiles = width // tile_cols
    row_band = band_table(row_taps, tile_cols + 2 * HALF, tile_cols)
    col_band = jnp.transpose(band_table(col_taps, p_rows + 2 * HALF, p_rows), (0, 2, 1))
    total_rows = p_rows * lax.axis_size("dec")
    total_cols = width * lax.axis_size("ra")
    ra_place = lax.axis_index("ra")
    rows_y = lax.axis_index("dec") * p_rows + jnp.arange(p_rows, dtype=jnp.int32)
    level = ((2 * rows_y + 1).astype(jnp.float32) / total_rows - 1.0)[None, :, None]

    def one_tile(tile_index, matched):
        start = tile_index * tile_cols
        slab = lax.dynamic_slice_in_dim(padded, start, tile_cols + 2 * HALF, 1)
        row_pass = jnp.einsum(
            "kcx,rc->kxr", row_band, slab, preferred_element_type=jnp.float32
        ).astype(jnp.bfloat16)
        col_pass = jnp.einsum(
            "kyr,kxr->kyx", col_band, row_pass, preferred_element_type=jnp.float32
        )
        cols_x = ra_place * width + start + jnp.arange(tile_cols, dtype=jnp.int32)
        phase = ((2 * cols_x + 1).astype(jnp.float32) * (math.pi / total_cols))[None, None, :]
        cosine = jnp.cos(phase)
        sine = jnp.sin(phase)
        field = (
            coef[:, 0, None, None]
            + coef[:, 1, None, None] * level
            + coef[:, 2, None, None] * (level * level)
            + coef[:, 3, None, None] * cosine
            + coef[:, 4, None, None] * sine
            + coef[:, 5, None, None] * (level * cosine)
        )
        return lax.dynamic_update_slice_in_dim(matched, jnp.sum(field * col_pass, axis=0), start, 1)

    matched = lax.fori_loop(0, n_tiles, one_tile, jnp.zeros((p_rows, width), jnp.float32))
    return science - matched


def solution(mesh):
    return jax.shard_map(
        local,
        mesh=mesh,
        in_specs=(
            P(("ra", "dec"), None),
            P(("ra", "dec"), None),
            P(("ra", "dec")),
            P("dec", "ra"),
            P(),
            P(),
            P(),
        ),
        out_specs=P("dec", "ra"),
        check_vma=False,
    )
```

profile of v0, /device:TPU:39, one launch (start us, length us, event | category | flops | bytes accessed | tf_op | source)
XLA Modules:
  0.0 166.8 jit_solution(4438681611509725100)
XLA Ops:
  0.0 0.8 compare_convert_fusion
  0.8 1.5 reduce-window.6
  2.7 0.7 fusion.24
  4.1 1.0 convert_reduce_fusion
  5.1 2.5 %collective-permute-start = (s32[128]{0:T(128)S(1)}, s32[128]{0:T(128)S(1)}, u32[]{:S(2)}, u32[]{:S(2)}) collective-permute-start(s32[128]{0:T(128)S(1)} %get-tuple-element.303), channel_id=1, source_target_pairs={{0,496},{8,504},{16,0},{24,8},{32,16},{40,24},{48,32},{56,40},{64,... | collective-permute-start | bytes 1544 | tf_op jit(solution)/shard_map/ppermute | solution.py:14
  7.6 2.9 %collective-permute-start.1 = (s32[128]{0:T(128)S(1)}, s32[128]{0:T(128)S(1)}, u32[]{:S(2)}, u32[]{:S(2)}) collective-permute-start(s32[128]{0:T(128)S(1)} %get-tuple-element.302), channel_id=1, source_target_pairs={{0,504},{8,0},{16,8},{24,16},{32,24},{40,32},{48,40},{56,48},{64,5... | collective-permute-start | bytes 1544 | tf_op jit(solution)/shard_map/ppermute | solution.py:14
  10.5 4.8 %collective-permute-start.2 = (s32[128]{0:T(128)S(1)}, s32[128]{0:T(128)S(1)}, u32[]{:S(2)}, u32[]{:S(2)}) collective-permute-start(s32[128]{0:T(128)S(1)} %get-tuple-element.301), channel_id=1, source_target_pairs={{0,8},{8,16},{16,24},{24,32},{32,40},{40,48},{48,56},{56,64},{64,7... | collective-permute-start | bytes 1544 | tf_op jit(solution)/shard_map/ppermute | solution.py:14
  15.3 2.8 %collective-permute-start.3 = (s32[128]{0:T(128)S(1)}, s32[128]{0:T(128)S(1)}, u32[]{:S(2)}, u32[]{:S(2)}) collective-permute-start(s32[128]{0:T(128)S(1)} %get-tuple-element.300), channel_id=1, source_target_pairs={{0,16},{8,24},{16,32},{24,40},{32,48},{40,56},{48,64},{56,72},{64,... | collective-permute-start | bytes 1544 | tf_op jit(solution)/shard_map/ppermute | solution.py:14
  18.1 4.7 %fusion.18 = f32[640,2048]{1,0:T(8,128)S(1)} fusion(f32[256,2048]{1,0:T(8,128)S(1)} %copy-done, s32[256]{0:T(256)S(1)} %multiply_add_fusion.3), kind=kOutput, calls=%fused_computation.37 | convolution fusion | flops 4027023360 | bytes 7341056 | tf_op jit(solution)/shard_map/dot_general | solution.py:55
  22.8 2.5 %fusion.27 = (f32[128,2048]{1,0:T(8,128)}, f32[128,2048]{1,0:T(8,128)}, f32[128,2048]{1,0:T(8,128)}, f32[128,2048]{1,0:T(8,128)}, f32[640,2048]{1,0:T(8,128)}) fusion(f32[640,2048]{1,0:T(8,128)S(1)} %fusion.18), kind=kLoop, calls=%fused_computation.67 | loop fusion | bytes 10485760 | tf_op jit(solution)/shard_map/slice | solution.py:67
  25.3 2.5 %collective-permute-start.4 = (f32[128,2048]{1,0:T(8,128)}, f32[128,2048]{1,0:T(8,128)}, u32[]{:S(2)}, u32[]{:S(2)}) collective-permute-start(f32[128,2048]{1,0:T(8,128)} %get-tuple-element.294), channel_id=1, source_target_pairs={{0,496},{8,504},{16,0},{24,8},{32,16},{40,24},{48,32},{56,40},{64,... | collective-permute-start | bytes 3145736 | tf_op jit(solution)/shard_map/ppermute | solution.py:14
  27.8 0.8 fusion.29
  28.6 2.0 %convert_bitcast_fusion = bf16[45,148,128]{2,0,1:T(8,128)(2,1)} fusion(s32[148,128]{1,0:T(8,128)S(1)} %iota_subtract_fusion, bf16[45,21]{0,1:T(8,128)(2,1)S(1)} %copy-done.3), kind=kOutput, calls=%fused_computation.27 | convolution fusion | flops 37054464 | bytes 1782626 | tf_op jit(solution)/shard_map/kq,qab->kab/dot_general | solution.py:38
  31.0 3.2 %copy.14 = bf16[45,148,128]{2,1,0:T(8,128)(2,1)} copy(bf16[45,148,128]{2,0,1:T(8,128)(2,1)} %convert_bitcast_fusion) | data formatting | bytes 3409920
  34.3 1.1 copy.15
  35.3 2.0 %collective-permute-start.5 = (f32[128,2048]{1,0:T(8,128)}, f32[128,2048]{1,0:T(8,128)}, u32[]{:S(2)}, u32[]{:S(2)}) collective-permute-start(f32[128,2048]{1,0:T(8,128)} %get-tuple-element.293), channel_id=1, source_target_pairs={{0,504},{8,0},{16,8},{24,16},{32,24},{40,32},{48,40},{56,48},{64,5... | collective-permute-start | bytes 3145736 | tf_op jit(solution)/shard_map/ppermute | solution.py:14
  37.4 5.8 %collective-permute-start.8 = (bf16[64,10]{1,0:T(8,128)(2,1)S(1)}, bf16[64,10]{1,0:T(8,128)(2,1)S(1)}, u32[]{:S(2)}, u32[]{:S(2)}) collective-permute-start(bf16[64,10]{1,0:T(8,128)(2,1)S(1)} %get-tuple-element.299), channel_id=1, source_target_pairs={{0,8},{8,16},{16,24},{24,32},{32,40},{40,48},{48,56},{56,64},{64,7... | collective-permute-start | bytes 3848 | tf_op jit(solution)/shard_map/ppermute | solution.py:24
  43.2 1.9 %collective-permute-start.9 = (bf16[64,10]{1,0:T(8,128)(2,1)S(1)}, bf16[64,10]{1,0:T(8,128)(2,1)S(1)}, u32[]{:S(2)}, u32[]{:S(2)}) collective-permute-start(bf16[64,10]{1,0:T(8,128)(2,1)S(1)} %get-tuple-element.298), channel_id=1, source_target_pairs={{8,0},{16,8},{24,16},{32,24},{40,32},{48,40},{56,48},{64,56},{72,6... | collective-permute-start | bytes 3848 | tf_op jit(solution)/shard_map/ppermute | solution.py:25
  45.1 5.8 %collective-permute-start.6 = (f32[128,2048]{1,0:T(8,128)}, f32[128,2048]{1,0:T(8,128)}, u32[]{:S(2)}, u32[]{:S(2)}) collective-permute-start(f32[128,2048]{1,0:T(8,128)} %get-tuple-element.292), channel_id=1, source_target_pairs={{0,8},{8,16},{16,24},{24,32},{32,40},{40,48},{48,56},{56,64},{64,7... | collective-permute-start | bytes 3145736 | tf_op jit(solution)/shard_map/ppermute | solution.py:14
  50.9 14.9 %collective-permute-done.9 = bf16[64,10]{1,0:T(8,128)(2,1)S(1)} collective-permute-done((bf16[64,10]{1,0:T(8,128)(2,1)S(1)}, bf16[64,10]{1,0:T(8,128)(2,1)S(1)}, u32[]{:S(2)}, u32[]{:S(2)}) %collective-permute-start.9) | collective-permute-done | bytes 1312 | tf_op jit(solution)/shard_map/ppermute | solution.py:25
  65.8 1.2 concatenate.14
  67.0 14.5 %collective-permute-start.10 = (bf16[10,2068]{1,0:T(8,128)(2,1)S(1)}, bf16[10,2068]{1,0:T(8,128)(2,1)S(1)}, u32[]{:S(2)}, u32[]{:S(2)}) collective-permute-start(bf16[10,2068]{1,0:T(8,128)(2,1)S(1)} %get-tuple-element.296), channel_id=1, source_target_pairs={{0,1},{1,2},{2,3},{3,4},{4,5},{5,6},{6,7},{8,9},{9,10},{10,11},{11... | collective-permute-start | bytes 124088 | tf_op jit(solution)/shard_map/ppermute | solution.py:24
  81.6 1.3 collective-permute-start.11
  83.0 2.7 %collective-permute-start.7 = (f32[128,2048]{1,0:T(8,128)}, f32[128,2048]{1,0:T(8,128)}, u32[]{:S(2)}, u32[]{:S(2)}) collective-permute-start(f32[128,2048]{1,0:T(8,128)} %get-tuple-element.291), channel_id=1, source_target_pairs={{0,16},{8,24},{16,32},{24,40},{32,48},{40,56},{48,64},{56,72},{64,... | collective-permute-start | bytes 3145736 | tf_op jit(solution)/shard_map/ppermute | solution.py:14
  85.7 21.7 %collective-permute-done.11 = bf16[10,2068]{1,0:T(8,128)(2,1)S(1)} collective-permute-done((bf16[10,2068]{1,0:T(8,128)(2,1)S(1)}, bf16[10,2068]{1,0:T(8,128)(2,1)S(1)}, u32[]{:S(2)}, u32[]{:S(2)}) %collective-permute-start.11) | collective-permute-done | bytes 41392 | tf_op jit(solution)/shard_map/ppermute | solution.py:25
  107.4 0.8 pad_maximum_fusion
  108.3 43.8 %while.17 = (s32[]{:T(128)}, f32[64,2048]{1,0:T(8,128)S(1)}, f32[45,6]{0,1:T(8,128)S(1)}, s32[]{:T(128)}, bf16[84,2068]{1,0:T(8,128)(2,1)}, /*index=5*/bf16[45,1...) while((s32[]{:T(128)}, f32[64,2048]{1,0:T(8,128)S(1)}, ...), condition=%wide.region_7.8_spmd.clone.clone, body=%wide.region_5.0_spmd.clone.clone.sunk | while | flops 207867968 | bytes 2566280 | solution.py:116
  108.7 2.3 %fusion.44 = f32[64,128]{1,0:T(8,128)S(1)} fusion(bf16[45,64,84]{2,1,0:T(8,128)(2,1)S(1)} %get-tuple-element.406, bf16[45,148,128]{2,1,0:T(8,128)(2,1)} %get-tuple-element.405, f32[64,128]{1,0:T(8,128)S(1)} %broadcast_multiply_fusion.6, f32[45]{0:T(128)S(1)} %get-tuple-element.366, f32[45,128]{1,0:T(8,128)S(1)} %broadcast_multiply_fusion.7, ...), kind=kOutput, calls=%fused_computation.4.clone.1 | convolution fusion | flops 207835648 | bytes 2403256 | tf_op jit(solution)/shard_map/while/body/eval_jaxpr/kyr,kxr->kyx/dot_general | solution.py:99
  111.5 2.3 %fusion.44 = f32[64,128]{1,0:T(8,128)S(1)} fusion(bf16[45,64,84]{2,1,0:T(8,128)(2,1)S(1)} %get-tuple-element.406, bf16[45,148,128]{2,1,0:T(8,128)(2,1)} %get-tuple-element.405, f32[64,128]{1,0:T(8,128)S(1)} %broadcast_multiply_fusion.6, f32[45]{0:T(128)S(1)} %get-tuple-element.366, f32[45,128]{1,0:T(8,128)S(1)} %broadcast_multiply_fusion.7, ...), kind=kOutput, calls=%fused_computation.4.clone.1 | convolution fusion | flops 207835648 | bytes 2403256 | tf_op jit(solution)/shard_map/while/body/eval_jaxpr/kyr,kxr->kyx/dot_general | solution.py:99
  114.2 2.3 %fusion.44 = f32[64,128]{1,0:T(8,128)S(1)} fusion(bf16[45,64,84]{2,1,0:T(8,128)(2,1)S(1)} %get-tuple-element.406, bf16[45,148,128]{2,1,0:T(8,128)(2,1)} %get-tuple-element.405, f32[64,128]{1,0:T(8,128)S(1)} %broadcast_multiply_fusion.6, f32[45]{0:T(128)S(1)} %get-tuple-element.366, f32[45,128]{1,0:T(8,128)S(1)} %broadcast_multiply_fusion.7, ...), kind=kOutput, calls=%fused_computation.4.clone.1 | convolution fusion | flops 207835648 | bytes 2403256 | tf_op jit(solution)/shard_map/while/body/eval_jaxpr/kyr,kxr->kyx/dot_general | solution.py:99
  116.9 2.3 %fusion.44 = f32[64,128]{1,0:T(8,128)S(1)} fusion(bf16[45,64,84]{2,1,0:T(8,128)(2,1)S(1)} %get-tuple-element.406, bf16[45,148,128]{2,1,0:T(8,128)(2,1)} %get-tuple-element.405, f32[64,128]{1,0:T(8,128)S(1)} %broadcast_multiply_fusion.6, f32[45]{0:T(128)S(1)} %get-tuple-element.366, f32[45,128]{1,0:T(8,128)S(1)} %broadcast_multiply_fusion.7, ...), kind=kOutput, calls=%fused_computation.4.clone.1 | convolution fusion | flops 207835648 | bytes 2403256 | tf_op jit(solution)/shard_map/while/body/eval_jaxpr/kyr,kxr->kyx/dot_general | solution.py:99
  119.7 2.3 %fusion.44 = f32[64,128]{1,0:T(8,128)S(1)} fusion(bf16[45,64,84]{2,1,0:T(8,128)(2,1)S(1)} %get-tuple-element.406, bf16[45,148,128]{2,1,0:T(8,128)(2,1)} %get-tuple-element.405, f32[64,128]{1,0:T(8,128)S(1)} %broadcast_multiply_fusion.6, f32[45]{0:T(128)S(1)} %get-tuple-element.366, f32[45,128]{1,0:T(8,128)S(1)} %broadcast_multiply_fusion.7, ...), kind=kOutput, calls=%fused_computation.4.clone.1 | convolution fusion | flops 207835648 | bytes 2403256 | tf_op jit(solution)/shard_map/while/body/eval_jaxpr/kyr,kxr->kyx/dot_general | solution.py:99
  122.4 2.3 %fusion.44 = f32[64,128]{1,0:T(8,128)S(1)} fusion(bf16[45,64,84]{2,1,0:T(8,128)(2,1)S(1)} %get-tuple-element.406, bf16[45,148,128]{2,1,0:T(8,128)(2,1)} %get-tuple-element.405, f32[64,128]{1,0:T(8,128)S(1)} %broadcast_multiply_fusion.6, f32[45]{0:T(128)S(1)} %get-tuple-element.366, f32[45,128]{1,0:T(8,128)S(1)} %broadcast_multiply_fusion.7, ...), kind=kOutput, calls=%fused_computation.4.clone.1 | convolution fusion | flops 207835648 | bytes 2403256 | tf_op jit(solution)/shard_map/while/body/eval_jaxpr/kyr,kxr->kyx/dot_general | solution.py:99
  125.2 2.3 %fusion.44 = f32[64,128]{1,0:T(8,128)S(1)} fusion(bf16[45,64,84]{2,1,0:T(8,128)(2,1)S(1)} %get-tuple-element.406, bf16[45,148,128]{2,1,0:T(8,128)(2,1)} %get-tuple-element.405, f32[64,128]{1,0:T(8,128)S(1)} %broadcast_multiply_fusion.6, f32[45]{0:T(128)S(1)} %get-tuple-element.366, f32[45,128]{1,0:T(8,128)S(1)} %broadcast_multiply_fusion.7, ...), kind=kOutput, calls=%fused_computation.4.clone.1 | convolution fusion | flops 207835648 | bytes 2403256 | tf_op jit(solution)/shard_map/while/body/eval_jaxpr/kyr,kxr->kyx/dot_general | solution.py:99
  127.9 2.3 %fusion.44 = f32[64,128]{1,0:T(8,128)S(1)} fusion(bf16[45,64,84]{2,1,0:T(8,128)(2,1)S(1)} %get-tuple-element.406, bf16[45,148,128]{2,1,0:T(8,128)(2,1)} %get-tuple-element.405, f32[64,128]{1,0:T(8,128)S(1)} %broadcast_multiply_fusion.6, f32[45]{0:T(128)S(1)} %get-tuple-element.366, f32[45,128]{1,0:T(8,128)S(1)} %broadcast_multiply_fusion.7, ...), kind=kOutput, calls=%fused_computation.4.clone.1 | convolution fusion | flops 207835648 | bytes 2403256 | tf_op jit(solution)/shard_map/while/body/eval_jaxpr/kyr,kxr->kyx/dot_general | solution.py:99
  130.6 2.3 %fusion.44 = f32[64,128]{1,0:T(8,128)S(1)} fusion(bf16[45,64,84]{2,1,0:T(8,128)(2,1)S(1)} %get-tuple-element.406, bf16[45,148,128]{2,1,0:T(8,128)(2,1)} %get-tuple-element.405, f32[64,128]{1,0:T(8,128)S(1)} %broadcast_multiply_fusion.6, f32[45]{0:T(128)S(1)} %get-tuple-element.366, f32[45,128]{1,0:T(8,128)S(1)} %broadcast_multiply_fusion.7, ...), kind=kOutput, calls=%fused_computation.4.clone.1 | convolution fusion | flops 207835648 | bytes 2403256 | tf_op jit(solution)/shard_map/while/body/eval_jaxpr/kyr,kxr->kyx/dot_general | solution.py:99
  133.4 2.3 %fusion.44 = f32[64,128]{1,0:T(8,128)S(1)} fusion(bf16[45,64,84]{2,1,0:T(8,128)(2,1)S(1)} %get-tuple-element.406, bf16[45,148,128]{2,1,0:T(8,128)(2,1)} %get-tuple-element.405, f32[64,128]{1,0:T(8,128)S(1)} %broadcast_multiply_fusion.6, f32[45]{0:T(128)S(1)} %get-tuple-element.366, f32[45,128]{1,0:T(8,128)S(1)} %broadcast_multiply_fusion.7, ...), kind=kOutput, calls=%fused_computation.4.clone.1 | convolution fusion | flops 207835648 | bytes 2403256 | tf_op jit(solution)/shard_map/while/body/eval_jaxpr/kyr,kxr->kyx/dot_general | solution.py:99
  136.1 2.3 %fusion.44 = f32[64,128]{1,0:T(8,128)S(1)} fusion(bf16[45,64,84]{2,1,0:T(8,128)(2,1)S(1)} %get-tuple-element.406, bf16[45,148,128]{2,1,0:T(8,128)(2,1)} %get-tuple-element.405, f32[64,128]{1,0:T(8,128)S(1)} %broadcast_multiply_fusion.6, f32[45]{0:T(128)S(1)} %get-tuple-element.366, f32[45,128]{1,0:T(8,128)S(1)} %broadcast_multiply_fusion.7, ...), kind=kOutput, calls=%fused_computation.4.clone.1 | convolution fusion | flops 207835648 | bytes 2403256 | tf_op jit(solution)/shard_map/while/body/eval_jaxpr/kyr,kxr->kyx/dot_general | solution.py:99
  138.9 2.3 %fusion.44 = f32[64,128]{1,0:T(8,128)S(1)} fusion(bf16[45,64,84]{2,1,0:T(8,128)(2,1)S(1)} %get-tuple-element.406, bf16[45,148,128]{2,1,0:T(8,128)(2,1)} %get-tuple-element.405, f32[64,128]{1,0:T(8,128)S(1)} %broadcast_multiply_fusion.6, f32[45]{0:T(128)S(1)} %get-tuple-element.366, f32[45,128]{1,0:T(8,128)S(1)} %broadcast_multiply_fusion.7, ...), kind=kOutput, calls=%fused_computation.4.clone.1 | convolution fusion | flops 207835648 | bytes 2403256 | tf_op jit(solution)/shard_map/while/body/eval_jaxpr/kyr,kxr->kyx/dot_general | solution.py:99
  141.6 2.3 %fusion.44 = f32[64,128]{1,0:T(8,128)S(1)} fusion(bf16[45,64,84]{2,1,0:T(8,128)(2,1)S(1)} %get-tuple-element.406, bf16[45,148,128]{2,1,0:T(8,128)(2,1)} %get-tuple-element.405, f32[64,128]{1,0:T(8,128)S(1)} %broadcast_multiply_fusion.6, f32[45]{0:T(128)S(1)} %get-tuple-element.366, f32[45,128]{1,0:T(8,128)S(1)} %broadcast_multiply_fusion.7, ...), kind=kOutput, calls=%fused_computation.4.clone.1 | convolution fusion | flops 207835648 | bytes 2403256 | tf_op jit(solution)/shard_map/while/body/eval_jaxpr/kyr,kxr->kyx/dot_general | solution.py:99
  144.3 2.3 %fusion.44 = f32[64,128]{1,0:T(8,128)S(1)} fusion(bf16[45,64,84]{2,1,0:T(8,128)(2,1)S(1)} %get-tuple-element.406, bf16[45,148,128]{2,1,0:T(8,128)(2,1)} %get-tuple-element.405, f32[64,128]{1,0:T(8,128)S(1)} %broadcast_multiply_fusion.6, f32[45]{0:T(128)S(1)} %get-tuple-element.366, f32[45,128]{1,0:T(8,128)S(1)} %broadcast_multiply_fusion.7, ...), kind=kOutput, calls=%fused_computation.4.clone.1 | convolution fusion | flops 207835648 | bytes 2403256 | tf_op jit(solution)/shard_map/while/body/eval_jaxpr/kyr,kxr->kyx/dot_general | solution.py:99
  147.1 2.3 %fusion.44 = f32[64,128]{1,0:T(8,128)S(1)} fusion(bf16[45,64,84]{2,1,0:T(8,128)(2,1)S(1)} %get-tuple-element.406, bf16[45,148,128]{2,1,0:T(8,128)(2,1)} %get-tuple-element.405, f32[64,128]{1,0:T(8,128)S(1)} %broadcast_multiply_fusion.6, f32[45]{0:T(128)S(1)} %get-tuple-element.366, f32[45,128]{1,0:T(8,128)S(1)} %broadcast_multiply_fusion.7, ...), kind=kOutput, calls=%fused_computation.4.clone.1 | convolution fusion | flops 207835648 | bytes 2403256 | tf_op jit(solution)/shard_map/while/body/eval_jaxpr/kyr,kxr->kyx/dot_general | solution.py:99
  149.8 2.3 %fusion.44 = f32[64,128]{1,0:T(8,128)S(1)} fusion(bf16[45,64,84]{2,1,0:T(8,128)(2,1)S(1)} %get-tuple-element.406, bf16[45,148,128]{2,1,0:T(8,128)(2,1)} %get-tuple-element.405, f32[64,128]{1,0:T(8,128)S(1)} %broadcast_multiply_fusion.6, f32[45]{0:T(128)S(1)} %get-tuple-element.366, f32[45,128]{1,0:T(8,128)S(1)} %broadcast_multiply_fusion.7, ...), kind=kOutput, calls=%fused_computation.4.clone.1 | convolution fusion | flops 207835648 | bytes 2403256 | tf_op jit(solution)/shard_map/while/body/eval_jaxpr/kyr,kxr->kyx/dot_general | solution.py:99
  152.2 2.4 %constant_dynamic-update-slice_fusion.5 = f32[640,2048]{1,0:T(8,128)} fusion(f32[640,2048]{1,0:T(8,128)} %get-tuple-element.295, f32[128,2048]{1,0:T(8,128)} %collective-permute-done.4), kind=kLoop, calls=%fused_computation.51 | loop fusion | bytes 2097152
  154.5 2.3 %constant_dynamic-update-slice_fusion.4 = f32[640,2048]{1,0:T(8,128)} fusion(f32[640,2048]{1,0:T(8,128)} %constant_dynamic-update-slice_fusion.5, f32[128,2048]{1,0:T(8,128)} %collective-permute-done.5), kind=kLoop, calls=%fused_computation.50 | loop fusion | bytes 2097152
  156.8 2.3 %constant_dynamic-update-slice_fusion.3 = f32[640,2048]{1,0:T(8,128)} fusion(f32[640,2048]{1,0:T(8,128)} %constant_dynamic-update-slice_fusion.4, f32[128,2048]{1,0:T(8,128)} %collective-permute-done.6), kind=kLoop, calls=%fused_computation.49 | loop fusion | bytes 2097152
  159.1 2.3 %constant_dynamic-update-slice_fusion.2 = f32[640,2048]{1,0:T(8,128)} fusion(f32[640,2048]{1,0:T(8,128)} %constant_dynamic-update-slice_fusion.3, f32[128,2048]{1,0:T(8,128)} %collective-permute-done.7), kind=kLoop, calls=%fused_computation.48 | loop fusion | bytes 2097152 | tf_op jit(solution)/shard_map/concatenate | solution.py:78
  161.4 5.4 %convolution_subtract_fusion = f32[64,2048]{1,0:T(8,128)} fusion(f32[64,2048]{1,0:T(8,128)S(1)} %get-tuple-element.202, f32[640,2048]{1,0:T(8,128)} %constant_dynamic-update-slice_fusion.2, s32[640]{0:T(1024)S(1)} %constant_dynamic-update-slice_fusion.6), kind=kOutput, calls=%fused_computation.26 | convolution fusion | flops 1006804992 | bytes 6294016 | tf_op jit(solution)/shard_map/dot_general | solution.py:76
  (167 shorter events, 7.7 us)
Async XLA Ops:
  0.0 18.1 %copy-start = (f32[256,2048]{1,0:T(8,128)S(1)}, f32[256,2048]{1,0:T(8,128)}, u32[]{:S(2)}) copy-start(f32[256,2048]{1,0:T(8,128)} %param.9) | copy-start | bytes 6291460
  5.1 30.2 %collective-permute-start = (s32[128]{0:T(128)S(1)}, s32[128]{0:T(128)S(1)}, u32[]{:S(2)}, u32[]{:S(2)}) collective-permute-start(s32[128]{0:T(128)S(1)} %get-tuple-element.303), channel_id=1, source_target_pairs={{0,496},{8,504},{16,0},{24,8},{32,16},{40,24},{48,32},{56,40},{64,... | collective-permute-start | bytes 1544 | tf_op jit(solution)/shard_map/ppermute | solution.py:14
  7.6 29.8 %collective-permute-start.1 = (s32[128]{0:T(128)S(1)}, s32[128]{0:T(128)S(1)}, u32[]{:S(2)}, u32[]{:S(2)}) collective-permute-start(s32[128]{0:T(128)S(1)} %get-tuple-element.302), channel_id=1, source_target_pairs={{0,504},{8,0},{16,8},{24,16},{32,24},{40,32},{48,40},{56,48},{64,5... | collective-permute-start | bytes 1544 | tf_op jit(solution)/shard_map/ppermute | solution.py:14
  10.5 32.7 %collective-permute-start.2 = (s32[128]{0:T(128)S(1)}, s32[128]{0:T(128)S(1)}, u32[]{:S(2)}, u32[]{:S(2)}) collective-permute-start(s32[128]{0:T(128)S(1)} %get-tuple-element.301), channel_id=1, source_target_pairs={{0,8},{8,16},{16,24},{24,32},{32,40},{40,48},{48,56},{56,64},{64,7... | collective-permute-start | bytes 1544 | tf_op jit(solution)/shard_map/ppermute | solution.py:14
  15.3 66.3 %collective-permute-start.3 = (s32[128]{0:T(128)S(1)}, s32[128]{0:T(128)S(1)}, u32[]{:S(2)}, u32[]{:S(2)}) collective-permute-start(s32[128]{0:T(128)S(1)} %get-tuple-element.300), channel_id=1, source_target_pairs={{0,16},{8,24},{16,32},{24,40},{32,48},{40,56},{48,64},{56,72},{64,... | collective-permute-start | bytes 1544 | tf_op jit(solution)/shard_map/ppermute | solution.py:14
  22.8 5.8 %copy-start.3 = (bf16[45,21]{0,1:T(8,128)(2,1)S(1)}, bf16[45,21]{0,1:T(8,128)(2,1)}, u32[]{:S(2)}) copy-start(bf16[45,21]{0,1:T(8,128)(2,1)} %param.13) | copy-start | bytes 5674
  22.8 7.8 %copy-start.4 = (bf16[45,21]{0,1:T(8,128)(2,1)S(1)}, bf16[45,21]{0,1:T(8,128)(2,1)}, u32[]{:S(2)}) copy-start(bf16[45,21]{0,1:T(8,128)(2,1)} %param.14) | copy-start | bytes 5674
  25.3 126.8 %collective-permute-start.4 = (f32[128,2048]{1,0:T(8,128)}, f32[128,2048]{1,0:T(8,128)}, u32[]{:S(2)}, u32[]{:S(2)}) collective-permute-start(f32[128,2048]{1,0:T(8,128)} %get-tuple-element.294), channel_id=1, source_target_pairs={{0,496},{8,504},{16,0},{24,8},{32,16},{40,24},{48,32},{56,40},{64,... | collective-permute-start | bytes 3145736 | tf_op jit(solution)/shard_map/ppermute | solution.py:14
  34.3 74.0 %copy-start.2 = (f32[45,6]{0,1:T(8,128)S(1)}, f32[45,6]{0,1:T(8,128)}, u32[]{:S(2)}) copy-start(f32[45,6]{0,1:T(8,128)} %param.15) | copy-start | bytes 3244
  35.3 73.0 %copy-start.1 = (bf16[45,64,84]{2,1,0:T(8,128)(2,1)S(1)}, bf16[45,64,84]{2,1,0:T(8,128)(2,1)}, u32[]{:S(2)}) copy-start(bf16[45,64,84]{2,1,0:T(8,128)(2,1)} %copy.15) | copy-start | bytes 1451524
  35.3 119.2 %collective-permute-start.5 = (f32[128,2048]{1,0:T(8,128)}, f32[128,2048]{1,0:T(8,128)}, u32[]{:S(2)}, u32[]{:S(2)}) collective-permute-start(f32[128,2048]{1,0:T(8,128)} %get-tuple-element.293), channel_id=1, source_target_pairs={{0,504},{8,0},{16,8},{24,16},{32,24},{40,32},{48,40},{56,48},{64,5... | collective-permute-start | bytes 3145736 | tf_op jit(solution)/shard_map/ppermute | solution.py:14
  37.4 7.7 %collective-permute-start.8 = (bf16[64,10]{1,0:T(8,128)(2,1)S(1)}, bf16[64,10]{1,0:T(8,128)(2,1)S(1)}, u32[]{:S(2)}, u32[]{:S(2)}) collective-permute-start(bf16[64,10]{1,0:T(8,128)(2,1)S(1)} %get-tuple-element.299), channel_id=1, source_target_pairs={{0,8},{8,16},{16,24},{24,32},{32,40},{40,48},{48,56},{56,64},{64,7... | collective-permute-start | bytes 3848 | tf_op jit(solution)/shard_map/ppermute | solution.py:24
  43.2 22.6 %collective-permute-start.9 = (bf16[64,10]{1,0:T(8,128)(2,1)S(1)}, bf16[64,10]{1,0:T(8,128)(2,1)S(1)}, u32[]{:S(2)}, u32[]{:S(2)}) collective-permute-start(bf16[64,10]{1,0:T(8,128)(2,1)S(1)} %get-tuple-element.298), channel_id=1, source_target_pairs={{8,0},{16,8},{24,16},{32,24},{40,32},{48,40},{56,48},{64,56},{72,6... | collective-permute-start | bytes 3848 | tf_op jit(solution)/shard_map/ppermute | solution.py:25
  45.1 111.7 %collective-permute-start.6 = (f32[128,2048]{1,0:T(8,128)}, f32[128,2048]{1,0:T(8,128)}, u32[]{:S(2)}, u32[]{:S(2)}) collective-permute-start(f32[128,2048]{1,0:T(8,128)} %get-tuple-element.292), channel_id=1, source_target_pairs={{0,8},{8,16},{16,24},{24,32},{32,40},{40,48},{48,56},{56,64},{64,7... | collective-permute-start | bytes 3145736 | tf_op jit(solution)/shard_map/ppermute | solution.py:14
  67.0 16.0 %collective-permute-start.10 = (bf16[10,2068]{1,0:T(8,128)(2,1)S(1)}, bf16[10,2068]{1,0:T(8,128)(2,1)S(1)}, u32[]{:S(2)}, u32[]{:S(2)}) collective-permute-start(bf16[10,2068]{1,0:T(8,128)(2,1)S(1)} %get-tuple-element.296), channel_id=1, source_target_pairs={{0,1},{1,2},{2,3},{3,4},{4,5},{5,6},{6,7},{8,9},{9,10},{10,11},{11... | collective-permute-start | bytes 124088 | tf_op jit(solution)/shard_map/ppermute | solution.py:24
  81.6 25.8 %collective-permute-start.11 = (bf16[10,2068]{1,0:T(8,128)(2,1)S(1)}, bf16[10,2068]{1,0:T(8,128)(2,1)S(1)}, u32[]{:S(2)}, u32[]{:S(2)}) collective-permute-start(bf16[10,2068]{1,0:T(8,128)(2,1)S(1)} %get-tuple-element.297), channel_id=1, source_target_pairs={{1,0},{2,1},{3,2},{4,3},{5,4},{6,5},{7,6},{9,8},{10,9},{11,10},{12... | collective-permute-start | bytes 124088 | tf_op jit(solution)/shard_map/ppermute | solution.py:25
  83.0 76.1 %collective-permute-start.7 = (f32[128,2048]{1,0:T(8,128)}, f32[128,2048]{1,0:T(8,128)}, u32[]{:S(2)}, u32[]{:S(2)}) collective-permute-start(f32[128,2048]{1,0:T(8,128)} %get-tuple-element.291), channel_id=1, source_target_pairs={{0,16},{8,24},{16,32},{24,40},{32,48},{40,56},{48,64},{56,72},{64,... | collective-permute-start | bytes 3145736 | tf_op jit(solution)/shard_map/ppermute | solution.py:14
where the time goes:
time: 168 us; the launch traced here: 167 us
  starting transfers between devices  49.4 us (29%)
  matrix products  49.2 us (29%)
  waiting for transfers between devices  36.7 us (22%)
  local copies, waits for them, and re-layouts  18.7 us (11%)
  other arithmetic  11.4 us (7%)
    dot_general x16, matrix products, one_tile(): jnp.einsum('kyr,kxr->kyx', col_band, row_pass, preferred_element_type=jnp...  36.7 us
    ppermute x2, waiting for transfers between devices, extended(): after = lax.ppermute(initial, axis, down)  36.6 us
    ppermute x8, starting transfers between devices, shifted(): lax.ppermute(value, axis, [(i, (i + by) % length) for i in range(length)])  25.9 us
    ppermute x2, starting transfers between devices, extended(): before = lax.ppermute(last, axis, up)  20.3 us
    unnamed x18, local copies, waits for them, and re-layouts  11.3 us
    dot_general x1, matrix products, local(): jnp.dot(placing, jnp.concatenate(arrived, axis=0), precision=lax.Precisio...  5.4 us
    dot_general x1, matrix products, local(): jnp.dot(select_int.astype(jnp.float32), exposure, precision=lax.Precision...  4.7 us
  transfers between devices with their start and end apart: 12, of which 3 were waited for; matrix products, arithmetic and copies ran while one was open for 40% of the time, Pallas kernels for 0%

commit v1 on v0

v1 whole, which is shorter than its diff:
```python
import functools
import math

import jax
import jax.numpy as jnp
from jax import lax
from jax.experimental import pallas as pl
from jax.experimental.pallas import tpu as pltpu
from jax.sharding import PartitionSpec as P

SPAN = 2
HALF = 10
TILE = 128
WIN = 256
ROWS_PAD = 96


def shifted(value, axis, by):
    length = lax.axis_size(axis)
    return lax.ppermute(value, axis, [(i, (i + by) % length) for i in range(length)])


def extended(value, sides, width, wrap):
    for axis, dim in sides:
        size, length = (lax.axis_size(axis), value.shape[dim])
        up = [(i, (i + 1) % size) for i in range(size if wrap else size - 1)]
        down = [(j, i) for i, j in up]
        last = lax.slice_in_dim(value, length - width, length, axis=dim)
        initial = lax.slice_in_dim(value, 0, width, axis=dim)
        before = lax.ppermute(last, axis, up)
        after = lax.ppermute(initial, axis, down)
        value = jnp.concatenate([before, value, after], axis=dim)
    return value


def row_band(row_taps, n_basis):
    taps = row_taps.shape[1]
    offset = jnp.arange(WIN, dtype=jnp.int32)[:, None] - jnp.arange(TILE, dtype=jnp.int32)[None, :]
    picks = (offset[None, :, :] == jnp.arange(taps, dtype=jnp.int32)[:, None, None]).astype(jnp.float32)
    band = jnp.einsum("kq,qct->ckt", row_taps.astype(jnp.float32), picks)
    band = jnp.pad(band, ((0, 0), (0, n_basis - row_taps.shape[0]), (0, 0)))
    return band.reshape(WIN, n_basis * TILE).astype(jnp.bfloat16)


def field_band(col_taps, coef, level, n_basis):
    k_count, taps = col_taps.shape
    p_rows = level.shape[0]
    offset = jnp.arange(ROWS_PAD, dtype=jnp.int32)[None, :] - jnp.arange(p_rows, dtype=jnp.int32)[:, None]
    picks = (offset[None, :, :] == jnp.arange(taps, dtype=jnp.int32)[:, None, None]).astype(jnp.float32)
    shifted_taps = jnp.einsum("kp,pyr->kyr", col_taps.astype(jnp.float32), picks)
    lv = level[None, :]
    plain = coef[:, 0, None] + coef[:, 1, None] * lv + coef[:, 2, None] * (lv * lv)
    with_cos = coef[:, 3, None] + coef[:, 5, None] * lv
    with_sin = jnp.broadcast_to(coef[:, 4, None], plain.shape)
    scale = jnp.stack([plain, with_cos, with_sin])
    weights = scale[:, :, :, None] * shifted_taps[None]
    weights = jnp.transpose(weights, (0, 2, 1, 3))
    weights = jnp.pad(weights, ((0, 0), (0, 0), (0, n_basis - k_count), (0, 0)))
    weights = weights.reshape(3 * p_rows, n_basis * ROWS_PAD)
    high = weights.astype(jnp.bfloat16)
    low = (weights - high.astype(jnp.float32)).astype(jnp.bfloat16)
    return jnp.concatenate([high, low], axis=0)


def conv_kernel(n_tiles, n_basis, p_rows, windows_ref, band_ref, weights_ref, trig_ref, out_ref, rp_ref):
    pair = 2 * TILE

    def row_step(step, carry):
        col = pl.multiple_of(step * pair, pair)
        part = jnp.dot(windows_ref[...], band_ref[:, pl.ds(col, pair)], preferred_element_type=jnp.float32)
        part = part.astype(jnp.bfloat16)
        for half in range(2):
            base = pl.multiple_of((2 * step + half) * ROWS_PAD, ROWS_PAD)
            for t in range(n_tiles):
                rp_ref[pl.ds(base, ROWS_PAD), t * TILE:(t + 1) * TILE] = part[
                    t * ROWS_PAD:(t + 1) * ROWS_PAD, half * TILE:(half + 1) * TILE
                ]
        return carry

    lax.fori_loop(0, n_basis // 2, row_step, 0)

    chunk = 256

    def col_step(step, carry):
        col = pl.multiple_of(step * chunk, chunk)
        sums = jnp.dot(weights_ref[...], rp_ref[:, pl.ds(col, chunk)], preferred_element_type=jnp.float32)
        lo = 3 * p_rows
        plain = sums[0:p_rows] + sums[lo:lo + p_rows]
        with_cos = sums[p_rows:2 * p_rows] + sums[lo + p_rows:lo + 2 * p_rows]
        with_sin = sums[2 * p_rows:3 * p_rows] + sums[lo + 2 * p_rows:lo + 3 * p_rows]
        cosine = trig_ref[0:1, pl.ds(col, chunk)]
        sine = trig_ref[1:2, pl.ds(col, chunk)]
        out_ref[:, pl.ds(col, chunk)] = plain + cosine * with_cos + sine * with_sin
        return carry

    lax.fori_loop(0, out_ref.shape[1] // chunk, col_step, 0)


def matched_template(padded, row_taps, col_taps, coef, level, trig):
    p_rows = level.shape[0]
    width = trig.shape[1]
    n_tiles = width // TILE
    n_basis = row_taps.shape[0] + (row_taps.shape[0] % 2)
    padded = jnp.pad(padded, ((0, ROWS_PAD - padded.shape[0]), (0, n_tiles * TILE + WIN - TILE - padded.shape[1])))
    windows = jnp.stack([padded[:, t * TILE:t * TILE + WIN] for t in range(n_tiles)]).reshape(n_tiles * ROWS_PAD, WIN)
    band = row_band(row_taps, n_basis)
    weights = field_band(col_taps, coef, level, n_basis)
    flops = 2 * n_tiles * ROWS_PAD * WIN * n_basis * TILE + 2 * weights.shape[0] * weights.shape[1] * width
    return pl.pallas_call(
        functools.partial(conv_kernel, n_tiles, n_basis, p_rows),
        out_shape=jax.ShapeDtypeStruct((p_rows, width), jnp.float32),
        in_specs=[pl.BlockSpec(memory_space=pltpu.VMEM)] * 4,
        out_specs=pl.BlockSpec(memory_space=pltpu.VMEM),
        scratch_shapes=[pltpu.VMEM((n_basis * ROWS_PAD, width), jnp.bfloat16)],
        compiler_params=pltpu.CompilerParams(vmem_limit_bytes=60 * 1024 * 1024),
        cost_estimate=pl.CostEstimate(flops=flops, transcendentals=0, bytes_accessed=8 * 1024 * 1024),
    )(windows, band, weights, trig)


def local(exposure, slots, target_rows, template, row_taps, col_taps, coef):
    e_rows, width = exposure.shape
    p_rows = template.shape[0]
    n_slots = 2 * SPAN + 1
    slot_ids = slots[:, 0]
    flat_place = slot_ids * p_rows + target_rows
    select = (jnp.arange(n_slots * p_rows, dtype=jnp.int32)[:, None] == flat_place[None, :]).astype(jnp.float32)
    partial = jnp.dot(
        select, exposure, precision=lax.Precision.HIGHEST, preferred_element_type=jnp.float32
    ).reshape(n_slots, p_rows, width)
    arrived = [partial[SPAN]]
    for offset in range(-SPAN, SPAN + 1):
        if offset != 0:
            arrived.append(shifted(partial[SPAN + offset], "ra", offset))

    widened = extended(template, (("ra", 1),), HALF, True)
    padded = extended(widened, (("dec", 0),), HALF, False)

    total_rows = p_rows * lax.axis_size("dec")
    total_cols = width * lax.axis_size("ra")
    rows_y = lax.axis_index("dec") * p_rows + jnp.arange(p_rows, dtype=jnp.int32)
    level = (2 * rows_y + 1).astype(jnp.float32) / total_rows - 1.0
    cols_x = lax.axis_index("ra") * width + jnp.arange(width, dtype=jnp.int32)
    phase = (2 * cols_x + 1).astype(jnp.float32) * (math.pi / total_cols)
    trig = jnp.stack([jnp.cos(phase), jnp.sin(phase)])

    matched = matched_template(padded, row_taps, col_taps, coef, level, trig)
    science = arrived[0]
    for part in arrived[1:]:
        science = science + part
    return science - matched


def solution(mesh):
    return jax.shard_map(
        local,
        mesh=mesh,
        in_specs=(
            P(("ra", "dec"), None),
            P(("ra", "dec"), None),
            P(("ra", "dec")),
            P("dec", "ra"),
            P(),
            P(),
            P(),
        ),
        out_specs=P("dec", "ra"),
        check_vma=False,
    )
```

time: 168 us -> 117 us (0.70)
  the two profiles are of different devices: /device:TPU:39 before, /device:TPU:511 now
where the time goes in v1:
time: 117 us; the launch traced here: 116 us
  starting transfers between devices  43.3 us (37%)
  local copies, waits for them, and re-layouts  28.7 us (25%)
  Pallas kernels  23.2 us (20%)
  other arithmetic  16.2 us (14%)
  matrix products  4.58 us (4%)
    pallas_call x1, Pallas kernels, matched_template(): pl.pallas_call(functools.partial(conv_kernel, n_tiles, n_basis, p_rows),...  23.2 us
    ppermute x4, starting transfers between devices, shifted(): lax.ppermute(value, axis, [(i, (i + by) % length) for i in range(length)])  19.8 us
    ppermute x2, starting transfers between devices, extended(): after = lax.ppermute(initial, axis, down)  15.2 us
    ppermute x2, starting transfers between devices, extended(): before = lax.ppermute(last, axis, up)  8.26 us
    unnamed x28, local copies, waits for them, and re-layouts  7.58 us
    reshape x1, local copies, waits for them, and re-layouts, field_band(): weights = weights.reshape(3 * p_rows, n_basis * ROWS_PAD)  5.76 us
    convert_element_type x1, other arithmetic, field_band(): low = (weights - high.astype(jnp.float32)).astype(jnp.bfloat16)  5.16 us
    convert_element_type x1, local copies, waits for them, and re-layouts, row_band(): return band.reshape(WIN, n_basis * TILE).astype(jnp.bfloat16)  4.67 us
  transfers between devices with their start and end apart: 8, of which 0 were waited for; matrix products, arithmetic and copies ran while one was open for 38% of the time, Pallas kernels for 20%

profile of v1, /device:TPU:511, one launch (start us, length us, event | category | flops | bytes accessed | tf_op | source)
XLA Modules:
  0.0 116.3 jit_solution(11239236154168094291)
XLA Ops:
  0.0 0.0 copy-start
  0.0 1.0 fusion.41
  1.0 7.0 %collective-permute-start.4 = (bf16[64,10]{1,0:T(8,128)(2,1)S(1)}, bf16[64,10]{1,0:T(8,128)(2,1)S(1)}, u32[]{:S(2)}, u32[]{:S(2)}) collective-permute-start(bf16[64,10]{1,0:T(8,128)(2,1)S(1)} %get-tuple-element.14), channel_id=1, source_target_pairs={{0,8},{8,16},{16,24},{24,32},{32,40},{40,48},{48,56},{56,64},{64,7... | collective-permute-start | bytes 3848 | tf_op jit(solution)/shard_map/ppermute | solution.py:30
  7.9 1.9 %collective-permute-start.5 = (bf16[64,10]{1,0:T(8,128)(2,1)S(1)}, bf16[64,10]{1,0:T(8,128)(2,1)S(1)}, u32[]{:S(2)}, u32[]{:S(2)}) collective-permute-start(bf16[64,10]{1,0:T(8,128)(2,1)S(1)} %get-tuple-element.13), channel_id=1, source_target_pairs={{8,0},{16,8},{24,16},{32,24},{40,32},{48,40},{56,48},{64,56},{72,6... | collective-permute-start | bytes 3848 | tf_op jit(solution)/shard_map/ppermute | solution.py:31
  9.9 0.7 broadcast_multiply_fusion.1
  10.6 0.7 add.133
  11.2 0.0 copy-done
  11.2 1.4 %fusion.16 = f32[320,2048]{1,0:T(8,128)S(1)} fusion(f32[256,2048]{1,0:T(8,128)S(1)} %copy-done, s32[256]{0:T(256)S(1)} %add.133), kind=kOutput, calls=%fused_computation.27 | convolution fusion | flops 2013347840 | bytes 4719616 | tf_op jit(solution)/shard_map/dot_general | solution.py:127
  12.7 0.0 copy-start.1
  12.7 1.5 %copy-done.1 = f32[320,2048]{1,0:T(8,128)} copy-done((f32[320,2048]{1,0:T(8,128)}, f32[320,2048]{1,0:T(8,128)S(1)}, u32[]{:S(2)}) %copy-start.1) | copy-done | bytes 2621464
  14.2 1.4 %fusion.39 = (f32[64,2048]{1,0:T(8,128)}, f32[64,2048]{1,0:T(8,128)}, f32[64,2048]{1,0:T(8,128)}, f32[64,2048]{1,0:T(8,128)}) fusion(f32[320,2048]{1,0:T(8,128)S(1)} %fusion.16), kind=kLoop, calls=%fused_computation.81 | loop fusion | bytes 4194304 | tf_op jit(solution)/shard_map/slice | solution.py:133
  15.5 1.9 %collective-permute-start = (f32[64,2048]{1,0:T(8,128)}, f32[64,2048]{1,0:T(8,128)S(1)}, u32[]{:S(2)}, u32[]{:S(2)}) collective-permute-start(f32[64,2048]{1,0:T(8,128)} %get-tuple-element.7), channel_id=1, source_target_pairs={{0,496},{8,504},{16,0},{24,8},{32,16},{40,24},{48,32},{56,40},{64,... | collective-permute-start | bytes 1572872 | tf_op jit(solution)/shard_map/ppermute | solution.py:20
  17.5 1.9 %collective-permute-start.1 = (f32[64,2048]{1,0:T(8,128)}, f32[64,2048]{1,0:T(8,128)S(1)}, u32[]{:S(2)}, u32[]{:S(2)}) collective-permute-start(f32[64,2048]{1,0:T(8,128)} %get-tuple-element.10), channel_id=1, source_target_pairs={{0,504},{8,0},{16,8},{24,16},{32,24},{40,32},{48,40},{56,48},{64,5... | collective-permute-start | bytes 1572872 | tf_op jit(solution)/shard_map/ppermute | solution.py:20
  19.4 12.4 %collective-permute-start.2 = (f32[64,2048]{1,0:T(8,128)}, f32[64,2048]{1,0:T(8,128)}, u32[]{:S(2)}, u32[]{:S(2)}) collective-permute-start(f32[64,2048]{1,0:T(8,128)} %get-tuple-element.9), channel_id=1, source_target_pairs={{0,8},{8,16},{16,24},{24,32},{32,40},{40,48},{48,56},{56,64},{64,7... | collective-permute-start | bytes 1572872 | tf_op jit(solution)/shard_map/ppermute | solution.py:20
  31.8 0.0 copy-done.5
  31.8 0.0 copy-done.2
  31.9 0.4 convolution_bitcast_fusion
  32.3 0.1 multiply_add_fusion.1
  32.4 1.4 %broadcast_multiply_fusion = f32[3,64,45,96]{3,2,1,0:T(8,128)S(1)} fusion(f32[64,45,96]{2,1,0:T(8,128)S(1)} %convolution_bitcast_fusion, f32[3,64,45]{2,1,0:T(8,128)S(1)} %maximum_bitcast_fusion), kind=kLoop, calls=%fused_computation.5 | loop fusion | flops 829440 | bytes 4458240 | tf_op jit(solution)/shard_map/mul | solution.py:56
  33.8 2.6 %pad.15 = f32[3,64,46,96]{3,2,1,0:T(8,128)} pad(f32[3,64,45,96]{3,2,1,0:T(8,128)S(1)} %broadcast_multiply_fusion, f32[]{:T(128)} %constant.29.clone.1), padding=0_0x0_0x0_1x0_0 | pad | bytes 6709252 | tf_op jit(solution)/shard_map/jit(_pad)/pad | solution.py:58
  36.4 5.8 %reshape.313 = f32[192,4416]{1,0:T(8,128)} reshape(f32[3,64,46,96]{3,2,1,0:T(8,128)} %pad.15) | data formatting | bytes 6782976 | tf_op jit(solution)/shard_map/reshape | solution.py:59
  42.2 5.2 %subtract_convert_fusion = (bf16[192,4416]{1,0:T(8,128)(2,1)}, bf16[192,4416]{1,0:T(8,128)(2,1)}) fusion(f32[192,4416]{1,0:T(8,128)} %reshape.313), kind=kLoop, calls=%fused_computation.1 | loop fusion | flops 3391488 | bytes 6782976 | tf_op jit(solution)/shard_map/convert_element_type | solution.py:61
  47.3 3.9 %pad_maximum_fusion.weights_ref = bf16[384,4416]{1,0:T(8,128)(2,1)} fusion(bf16[192,4416]{1,0:T(8,128)(2,1)} %get-tuple-element.5, bf16[192,4416]{1,0:T(8,128)(2,1)} %get-tuple-element.6), kind=kLoop, calls=%fused_computation | loop fusion | flops 6782976 | bytes 6782976 | tf_op jit(solution)/shard_map/concatenate | solution.py:62
  51.3 0.0 copy-done.3
  51.3 2.7 %convert_bitcast_fusion = bf16[256,45,128]{2,1,0:T(8,128)(2,1)} fusion(s32[256,128]{1,0:T(8,128)S(1)} %iota_subtract_fusion, bf16[45,21]{0,1:T(8,128)(2,1)S(1)} %copy-done.3), kind=kOutput, calls=%fused_computation.2 | convolution fusion | flops 64094208 | bytes 3082082 | tf_op jit(solution)/shard_map/kq,qct->ckt/dot_general | solution.py:40
  54.0 0.3 fusion.36
  54.3 0.0 collective-permute-done.4
  54.3 0.0 collective-permute-done.5
  54.3 1.2 %concatenate.9 = bf16[64,2068]{1,0:T(8,128)(2,1)S(1)} concatenate(bf16[64,10]{1,0:T(8,128)(2,1)S(1)} %collective-permute-done.4, bf16[64,2048]{1,0:T(8,128)(2,1)} %param.10, bf16[64,10]{1,0:T(8,128)(2,1)S(1)} %collective-permute-done.5), dimensions={1} | concatenate | bytes 529408 | tf_op jit(solution)/shard_map/concatenate | solution.py:32
  55.5 0.7 fusion.40
  56.2 1.3 %collective-permute-start.6 = (bf16[10,2068]{1,0:T(8,128)(2,1)}, bf16[10,2068]{1,0:T(8,128)(2,1)S(1)}, u32[]{:S(2)}, u32[]{:S(2)}) collective-permute-start(bf16[10,2068]{1,0:T(8,128)(2,1)} %get-tuple-element.11), channel_id=1, source_target_pairs={{0,1},{1,2},{2,3},{3,4},{4,5},{5,6},{6,7},{8,9},{9,10},{10,11},{11... | collective-permute-start | bytes 124088 | tf_op jit(solution)/shard_map/ppermute | solution.py:30
  57.5 13.3 %collective-permute-start.7 = (bf16[10,2068]{1,0:T(8,128)(2,1)}, bf16[10,2068]{1,0:T(8,128)(2,1)}, u32[]{:S(2)}, u32[]{:S(2)}) collective-permute-start(bf16[10,2068]{1,0:T(8,128)(2,1)} %get-tuple-element.12), channel_id=1, source_target_pairs={{1,0},{2,1},{3,2},{4,3},{5,4},{6,5},{7,6},{9,8},{10,9},{11,10},{12... | collective-permute-start | bytes 124088 | tf_op jit(solution)/shard_map/ppermute | solution.py:31
  70.8 0.6 pad_maximum_fusion.1.trig_ref
  71.4 5.1 %copy.10 = bf16[256,45,128]{0,2,1:T(8,128)(2,1)} copy(bf16[256,45,128]{2,1,0:T(8,128)(2,1)} %convert_bitcast_fusion) | data formatting | bytes 5898240
  76.5 3.9 %pad.14.clone = bf16[256,46,128]{0,2,1:T(8,128)(2,1)} pad(bf16[256,45,128]{0,2,1:T(8,128)(2,1)} %copy.10, bf16[]{:T(256)} %constant.13.clone.1), padding=0_0x0_1x0_0 | pad | bytes 5963778 | tf_op jit(solution)/shard_map/jit(_pad)/pad | solution.py:41
  80.4 4.7 %copy.9.band_ref = bf16[256,5888]{1,0:T(8,128)(2,1)} copy(bf16[256,5888]{0,1:T(8,128)(2,1)} %bitcast.92) | data formatting | bytes 6029312 | tf_op jit(solution)/shard_map/convert_element_type | solution.py:42
  85.1 0.0 collective-permute-done.6
  85.1 3.6 %collective-permute-start.3 = (f32[64,2048]{1,0:T(8,128)}, f32[64,2048]{1,0:T(8,128)S(1)}, u32[]{:S(2)}, u32[]{:S(2)}) collective-permute-start(f32[64,2048]{1,0:T(8,128)} %get-tuple-element.8), channel_id=1, source_target_pairs={{0,16},{8,24},{16,32},{24,40},{32,48},{40,56},{48,64},{56,72},{64,... | collective-permute-start | bytes 1572872 | tf_op jit(solution)/shard_map/ppermute | solution.py:20
  88.7 0.0 collective-permute-done.7
  88.7 1.0 fusion.14
  89.9 0.0 copy-start.4
  89.9 0.9 copy-done.4
  90.8 23.2 %shard_map.73 = f32[64,2048]{1,0:T(8,128)} custom-call(bf16[1536,256]{1,0:T(8,128)(2,1)} %bitcast.94, bf16[256,5888]{1,0:T(8,128)(2,1)} %copy.9.band_ref, bf16[384,4416]{1,0:T(8,128)(2,1)} %pad_maximum_fusion.weights_ref, f32[2,2048]{1,0:T(2,128)} %pad_maximum_fusion.1.trig_ref), custom_call_target="tpu_custom_call" | custom-call | flops 11576279040 | bytes 8388608 | tf_op jit(solution)/shard_map/pallas_call | solution.py:109
  114.0 0.0 collective-permute-done
  114.0 0.0 collective-permute-done.1
  114.0 0.0 collective-permute-done.2
  114.0 0.0 collective-permute-done.3
  114.0 2.3 %fusion.9 = f32[64,2048]{1,0:T(8,128)} fusion(f32[64,2048]{1,0:T(8,128)} %shard_map.73, f32[64,2048]{1,0:T(8,128)S(1)} %collective-permute-done.3, f32[64,2048]{1,0:T(8,128)} %collective-permute-done.2, f32[64,2048]{1,0:T(8,128)S(1)} %collective-permute-done.1, f32[64,2048]{1,0:T(8,128)S(1)} %collective-permute-done, f32[320,2048]{1,0:T(8,128)} %copy-done.1), kind=kLoop, calls=%fused_computation.19 | loop fusion | flops 655360 | bytes 3670016 | tf_op jit(solution)/shard_map/sub | solution.py:150
  (25 shorter events, 0.2 us)
Async XLA Ops:
  0.0 11.2 %copy-start = (f32[256,2048]{1,0:T(8,128)S(1)}, f32[256,2048]{1,0:T(8,128)}, u32[]{:S(2)}) copy-start(f32[256,2048]{1,0:T(8,128)} %param.7) | copy-start | bytes 6291460
  1.0 53.3 %collective-permute-start.4 = (bf16[64,10]{1,0:T(8,128)(2,1)S(1)}, bf16[64,10]{1,0:T(8,128)(2,1)S(1)}, u32[]{:S(2)}, u32[]{:S(2)}) collective-permute-start(bf16[64,10]{1,0:T(8,128)(2,1)S(1)} %get-tuple-element.14), channel_id=1, source_target_pairs={{0,8},{8,16},{16,24},{24,32},{32,40},{40,48},{48,56},{56,64},{64,7... | collective-permute-start | bytes 3848 | tf_op jit(solution)/shard_map/ppermute | solution.py:30
  7.9 46.4 %collective-permute-start.5 = (bf16[64,10]{1,0:T(8,128)(2,1)S(1)}, bf16[64,10]{1,0:T(8,128)(2,1)S(1)}, u32[]{:S(2)}, u32[]{:S(2)}) collective-permute-start(bf16[64,10]{1,0:T(8,128)(2,1)S(1)} %get-tuple-element.13), channel_id=1, source_target_pairs={{8,0},{16,8},{24,16},{32,24},{40,32},{48,40},{56,48},{64,56},{72,6... | collective-permute-start | bytes 3848 | tf_op jit(solution)/shard_map/ppermute | solution.py:31
  12.7 1.5 %copy-start.1 = (f32[320,2048]{1,0:T(8,128)}, f32[320,2048]{1,0:T(8,128)S(1)}, u32[]{:S(2)}) copy-start(f32[320,2048]{1,0:T(8,128)S(1)} %fusion.16) | copy-start | bytes 7864324
  14.2 17.6 %copy-start.5 = (f32[45,6]{0,1:T(8,128)S(1)}, f32[45,6]{0,1:T(8,128)}, u32[]{:S(2)}) copy-start(f32[45,6]{0,1:T(8,128)} %param.13) | copy-start | bytes 3244
  14.2 17.7 %copy-start.2 = (bf16[45,21]{0,1:T(8,128)(2,1)S(1)}, bf16[45,21]{0,1:T(8,128)(2,1)}, u32[]{:S(2)}) copy-start(bf16[45,21]{0,1:T(8,128)(2,1)} %param.12) | copy-start | bytes 5674
  15.5 98.4 %collective-permute-start = (f32[64,2048]{1,0:T(8,128)}, f32[64,2048]{1,0:T(8,128)S(1)}, u32[]{:S(2)}, u32[]{:S(2)}) collective-permute-start(f32[64,2048]{1,0:T(8,128)} %get-tuple-element.7), channel_id=1, source_target_pairs={{0,496},{8,504},{16,0},{24,8},{32,16},{40,24},{48,32},{56,40},{64,... | collective-permute-start | bytes 1572872 | tf_op jit(solution)/shard_map/ppermute | solution.py:20
  17.5 96.5 %collective-permute-start.1 = (f32[64,2048]{1,0:T(8,128)}, f32[64,2048]{1,0:T(8,128)S(1)}, u32[]{:S(2)}, u32[]{:S(2)}) collective-permute-start(f32[64,2048]{1,0:T(8,128)} %get-tuple-element.10), channel_id=1, source_target_pairs={{0,504},{8,0},{16,8},{24,16},{32,24},{40,32},{48,40},{56,48},{64,5... | collective-permute-start | bytes 1572872 | tf_op jit(solution)/shard_map/ppermute | solution.py:20
  19.4 94.6 %collective-permute-start.2 = (f32[64,2048]{1,0:T(8,128)}, f32[64,2048]{1,0:T(8,128)}, u32[]{:S(2)}, u32[]{:S(2)}) collective-permute-start(f32[64,2048]{1,0:T(8,128)} %get-tuple-element.9), channel_id=1, source_target_pairs={{0,8},{8,16},{16,24},{24,32},{32,40},{40,48},{48,56},{56,64},{64,7... | collective-permute-start | bytes 1572872 | tf_op jit(solution)/shard_map/ppermute | solution.py:20
  47.3 3.9 %copy-start.3 = (bf16[45,21]{0,1:T(8,128)(2,1)S(1)}, bf16[45,21]{0,1:T(8,128)(2,1)}, u32[]{:S(2)}) copy-start(bf16[45,21]{0,1:T(8,128)(2,1)} %param.11) | copy-start | bytes 5674
  56.2 28.9 %collective-permute-start.6 = (bf16[10,2068]{1,0:T(8,128)(2,1)}, bf16[10,2068]{1,0:T(8,128)(2,1)S(1)}, u32[]{:S(2)}, u32[]{:S(2)}) collective-permute-start(bf16[10,2068]{1,0:T(8,128)(2,1)} %get-tuple-element.11), channel_id=1, source_target_pairs={{0,1},{1,2},{2,3},{3,4},{4,5},{5,6},{6,7},{8,9},{9,10},{10,11},{11... | collective-permute-start | bytes 124088 | tf_op jit(solution)/shard_map/ppermute | solution.py:30
  57.5 31.2 %collective-permute-start.7 = (bf16[10,2068]{1,0:T(8,128)(2,1)}, bf16[10,2068]{1,0:T(8,128)(2,1)}, u32[]{:S(2)}, u32[]{:S(2)}) collective-permute-start(bf16[10,2068]{1,0:T(8,128)(2,1)} %get-tuple-element.12), channel_id=1, source_target_pairs={{1,0},{2,1},{3,2},{4,3},{5,4},{6,5},{7,6},{9,8},{10,9},{11,10},{12... | collective-permute-start | bytes 124088 | tf_op jit(solution)/shard_map/ppermute | solution.py:31
  85.1 28.9 %collective-permute-start.3 = (f32[64,2048]{1,0:T(8,128)}, f32[64,2048]{1,0:T(8,128)S(1)}, u32[]{:S(2)}, u32[]{:S(2)}) collective-permute-start(f32[64,2048]{1,0:T(8,128)} %get-tuple-element.8), channel_id=1, source_target_pairs={{0,16},{8,24},{16,32},{24,40},{32,48},{40,56},{48,64},{56,72},{64,... | collective-permute-start | bytes 1572872 | tf_op jit(solution)/shard_map/ppermute | solution.py:20
  89.9 0.9 copy-start.4

commit v2 on v1

--- a/solution.py
+++ b/solution.py
@@ -36,38 +36,38 @@
 def row_band(row_taps, n_basis):
     taps = row_taps.shape[1]
     offset = jnp.arange(WIN, dtype=jnp.int32)[:, None] - jnp.arange(TILE, dtype=jnp.int32)[None, :]
-    picks = (offset[None, :, :] == jnp.arange(taps, dtype=jnp.int32)[:, None, None]).astype(jnp.float32)
-    band = jnp.einsum("kq,qct->ckt", row_taps.astype(jnp.float32), picks)
-    band = jnp.pad(band, ((0, 0), (0, n_basis - row_taps.shape[0]), (0, 0)))
-    return band.reshape(WIN, n_basis * TILE).astype(jnp.bfloat16)
+    picks = (offset[None, :, :] == jnp.arange(taps, dtype=jnp.int32)[:, None, None]).astype(jnp.bfloat16)
+    padded_taps = jnp.pad(row_taps, ((0, n_basis - row_taps.shape[0]), (0, 0)))
+    band = jnp.dot(padded_taps, picks.reshape(taps, WIN * TILE), preferred_element_type=jnp.float32)
+    return band.astype(jnp.bfloat16).reshape(n_basis, WIN, TILE)
 
 
 def field_band(col_taps, coef, level, n_basis):
     k_count, taps = col_taps.shape
     p_rows = level.shape[0]
     offset = jnp.arange(ROWS_PAD, dtype=jnp.int32)[None, :] - jnp.arange(p_rows, dtype=jnp.int32)[:, None]
-    picks = (offset[None, :, :] == jnp.arange(taps, dtype=jnp.int32)[:, None, None]).astype(jnp.float32)
-    shifted_taps = jnp.einsum("kp,pyr->kyr", col_taps.astype(jnp.float32), picks)
-    lv = level[None, :]
-    plain = coef[:, 0, None] + coef[:, 1, None] * lv + coef[:, 2, None] * (lv * lv)
-    with_cos = coef[:, 3, None] + coef[:, 5, None] * lv
-    with_sin = jnp.broadcast_to(coef[:, 4, None], plain.shape)
+    picks = (offset[:, None, :] == jnp.arange(taps, dtype=jnp.int32)[None, :, None]).astype(jnp.float32)
+    taps_f = jnp.pad(col_taps.astype(jnp.float32), ((0, n_basis - k_count), (0, 0)))
+    shifted_taps = jnp.einsum("kp,ypr->ykr", taps_f, picks)
+    coef = jnp.pad(coef, ((0, n_basis - k_count), (0, 0)))
+    lv = level[:, None]
+    plain = coef[None, :, 0] + coef[None, :, 1] * lv + coef[None, :, 2] * (lv * lv)
+    with_cos = coef[None, :, 3] + coef[None, :, 5] * lv
+    with_sin = jnp.broadcast_to(coef[None, :, 4], plain.shape)
     scale = jnp.stack([plain, with_cos, with_sin])
-    weights = scale[:, :, :, None] * shifted_taps[None]
-    weights = jnp.transpose(weights, (0, 2, 1, 3))
-    weights = jnp.pad(weights, ((0, 0), (0, 0), (0, n_basis - k_count), (0, 0)))
-    weights = weights.reshape(3 * p_rows, n_basis * ROWS_PAD)
-    high = weights.astype(jnp.bfloat16)
-    low = (weights - high.astype(jnp.float32)).astype(jnp.bfloat16)
-    return jnp.concatenate([high, low], axis=0)
+    weights = (scale[:, :, :, None] * shifted_taps[None]).reshape(3 * p_rows, n_basis * ROWS_PAD)
+    high = lax.reduce_precision(weights, exponent_bits=8, mantissa_bits=7)
+    low = weights - high
+    return jnp.concatenate([high.astype(jnp.bfloat16), low.astype(jnp.bfloat16)], axis=0)
 
 
-def conv_kernel(n_tiles, n_basis, p_rows, windows_ref, band_ref, weights_ref, trig_ref, out_ref, rp_ref):
-    pair = 2 * TILE
+def conv_kernel(n_tiles, n_basis, p_rows, padded_ref, band_ref, weights_ref, trig_ref, out_ref, rp_ref, windows_ref):
+    for t in range(n_tiles):
+        windows_ref[t * ROWS_PAD:(t + 1) * ROWS_PAD, :] = padded_ref[:, t * TILE:t * TILE + WIN]
 
     def row_step(step, carry):
-        col = pl.multiple_of(step * pair, pair)
-        part = jnp.dot(windows_ref[...], band_ref[:, pl.ds(col, pair)], preferred_element_type=jnp.float32)
+        rhs = jnp.concatenate([band_ref[2 * step], band_ref[2 * step + 1]], axis=1)
+        part = jnp.dot(windows_ref[...], rhs, preferred_element_type=jnp.float32)
         part = part.astype(jnp.bfloat16)
         for half in range(2):
             base = pl.multiple_of((2 * step + half) * ROWS_PAD, ROWS_PAD)
@@ -102,7 +102,6 @@
     n_tiles = width // TILE
     n_basis = row_taps.shape[0] + (row_taps.shape[0] % 2)
     padded = jnp.pad(padded, ((0, ROWS_PAD - padded.shape[0]), (0, n_tiles * TILE + WIN - TILE - padded.shape[1])))
-    windows = jnp.stack([padded[:, t * TILE:t * TILE + WIN] for t in range(n_tiles)]).reshape(n_tiles * ROWS_PAD, WIN)
     band = row_band(row_taps, n_basis)
     weights = field_band(col_taps, coef, level, n_basis)
     flops = 2 * n_tiles * ROWS_PAD * WIN * n_basis * TILE + 2 * weights.shape[0] * weights.shape[1] * width
@@ -111,10 +110,13 @@
         out_shape=jax.ShapeDtypeStruct((p_rows, width), jnp.float32),
         in_specs=[pl.BlockSpec(memory_space=pltpu.VMEM)] * 4,
         out_specs=pl.BlockSpec(memory_space=pltpu.VMEM),
-        scratch_shapes=[pltpu.VMEM((n_basis * ROWS_PAD, width), jnp.bfloat16)],
+        scratch_shapes=[
+            pltpu.VMEM((n_basis * ROWS_PAD, width), jnp.bfloat16),
+            pltpu.VMEM((n_tiles * ROWS_PAD, WIN), jnp.bfloat16),
+        ],
         compiler_params=pltpu.CompilerParams(vmem_limit_bytes=60 * 1024 * 1024),
         cost_estimate=pl.CostEstimate(flops=flops, transcendentals=0, bytes_accessed=8 * 1024 * 1024),
-    )(windows, band, weights, trig)
+    )(padded, band, weights, trig)
 
 
 def local(exposure, slots, target_rows, template, row_taps, col_taps, coef):

time: 117 us -> 108 us (0.923)
  the two profiles are of different devices: /device:TPU:511 before, /device:TPU:1 now
where the time goes in v2:
time: 108 us
  starting transfers between devices  41.8 us (39%)
  Pallas kernels  23.1 us (21%)
  other arithmetic  17.1 us (16%)
  local copies, waits for them, and re-layouts  15.6 us (14%)
  waiting for transfers between devices  5.55 us (5%)
  matrix products  4.52 us (4%)
    pallas_call x1, Pallas kernels, matched_template(): pl.pallas_call(functools.partial(conv_kernel, n_tiles, n_basis, p_rows),...  23.1 us
    ppermute x4, starting transfers between devices, shifted(): lax.ppermute(value, axis, [(i, (i + by) % length) for i in range(length)])  19.8 us
    ppermute x2, starting transfers between devices, extended(): before = lax.ppermute(last, axis, up)  14.5 us
    ppermute x2, starting transfers between devices, extended(): after = lax.ppermute(initial, axis, down)  7.49 us
    mul x1, local copies, waits for them, and re-layouts, field_band(): scale[:, :, :, None] * shifted_taps[None]  5.83 us
    ppermute x2, waiting for transfers between devices, extended(): after = lax.ppermute(initial, axis, down)  5.53 us
    unnamed x11, local copies, waits for them, and re-layouts  4.18 us
    convert_element_type x1, other arithmetic, field_band(): high.astype(jnp.bfloat16)  4.05 us
  transfers between devices with their start and end apart: 8, of which 1 were waited for; matrix products, arithmetic and copies ran while one was open for 30% of the time, Pallas kernels for 21%

profile of v2, /device:TPU:1, one launch (start us, length us, event | category | flops | bytes accessed | tf_op | source)
XLA Modules:
  0.0 107.9 jit_solution(5994118259238015028)
XLA Ops:
  0.0 0.0 copy-start
  0.0 1.0 fusion.34
  1.0 4.5 %collective-permute-start.4 = (bf16[64,10]{1,0:T(8,128)(2,1)S(1)}, bf16[64,10]{1,0:T(8,128)(2,1)S(1)}, u32[]{:S(2)}, u32[]{:S(2)}) collective-permute-start(bf16[64,10]{1,0:T(8,128)(2,1)S(1)} %get-tuple-element.14), channel_id=1, source_target_pairs={{0,8},{8,16},{16,24},{24,32},{32,40},{40,48},{48,56},{56,64},{64,7... | collective-permute-start | bytes 3848 | tf_op jit(solution)/shard_map/ppermute | solution.py:30
  5.5 6.2 %collective-permute-start.5 = (bf16[64,10]{1,0:T(8,128)(2,1)S(1)}, bf16[64,10]{1,0:T(8,128)(2,1)S(1)}, u32[]{:S(2)}, u32[]{:S(2)}) collective-permute-start(bf16[64,10]{1,0:T(8,128)(2,1)S(1)} %get-tuple-element.13), channel_id=1, source_target_pairs={{8,0},{16,8},{24,16},{32,24},{40,32},{48,40},{56,48},{64,56},{72,6... | collective-permute-start | bytes 3848 | tf_op jit(solution)/shard_map/ppermute | solution.py:31
  11.7 0.7 broadcast_multiply_fusion.1
  12.4 0.7 add.135
  13.0 0.0 copy-done
  13.0 1.4 %fusion.16 = f32[320,2048]{1,0:T(8,128)S(1)} fusion(f32[256,2048]{1,0:T(8,128)S(1)} %copy-done, s32[256]{0:T(256)S(1)} %add.135), kind=kOutput, calls=%fused_computation.28 | convolution fusion | flops 2013347840 | bytes 4719616 | tf_op jit(solution)/shard_map/dot_general | solution.py:129
  14.5 0.0 copy-start.1
  14.5 1.5 %copy-done.1 = f32[320,2048]{1,0:T(8,128)} copy-done((f32[320,2048]{1,0:T(8,128)}, f32[320,2048]{1,0:T(8,128)S(1)}, u32[]{:S(2)}) %copy-start.1) | copy-done | bytes 2621464
  16.0 0.0 copy-start.4
  16.0 0.0 copy-start.2
  16.0 1.4 %fusion.32 = (f32[64,2048]{1,0:T(8,128)}, f32[64,2048]{1,0:T(8,128)}, f32[64,2048]{1,0:T(8,128)}, f32[64,2048]{1,0:T(8,128)}) fusion(f32[320,2048]{1,0:T(8,128)S(1)} %fusion.16), kind=kLoop, calls=%fused_computation.59 | loop fusion | bytes 4194304 | tf_op jit(solution)/shard_map/slice | solution.py:135
  17.4 12.0 %collective-permute-start = (f32[64,2048]{1,0:T(8,128)}, f32[64,2048]{1,0:T(8,128)S(1)}, u32[]{:S(2)}, u32[]{:S(2)}) collective-permute-start(f32[64,2048]{1,0:T(8,128)} %get-tuple-element.7), channel_id=1, source_target_pairs={{0,496},{8,504},{16,0},{24,8},{32,16},{40,24},{48,32},{56,40},{64,... | collective-permute-start | bytes 1572872 | tf_op jit(solution)/shard_map/ppermute | solution.py:20
  29.3 2.3 %collective-permute-start.1 = (f32[64,2048]{1,0:T(8,128)}, f32[64,2048]{1,0:T(8,128)S(1)}, u32[]{:S(2)}, u32[]{:S(2)}) collective-permute-start(f32[64,2048]{1,0:T(8,128)} %get-tuple-element.10), channel_id=1, source_target_pairs={{0,504},{8,0},{16,8},{24,16},{32,24},{40,32},{48,40},{56,48},{64,5... | collective-permute-start | bytes 1572872 | tf_op jit(solution)/shard_map/ppermute | solution.py:20
  31.7 3.5 %collective-permute-start.2 = (f32[64,2048]{1,0:T(8,128)}, f32[64,2048]{1,0:T(8,128)}, u32[]{:S(2)}, u32[]{:S(2)}) collective-permute-start(f32[64,2048]{1,0:T(8,128)} %get-tuple-element.9), channel_id=1, source_target_pairs={{0,8},{8,16},{16,24},{24,32},{32,40},{40,48},{48,56},{56,64},{64,7... | collective-permute-start | bytes 1572872 | tf_op jit(solution)/shard_map/ppermute | solution.py:20
  35.2 0.0 copy-done.4
  35.3 0.0 copy-done.2
  35.3 0.4 convolution_bitcast_fusion
  35.7 0.1 multiply_add_fusion.1
  35.8 3.4 %broadcast_multiply_fusion = f32[3,64,46,96]{3,2,1,0:T(8,128)} fusion(f32[64,46,96]{2,1,0:T(8,128)S(1)} %convolution_bitcast_fusion, f32[3,64,46]{2,1,0:T(8,128)S(1)} %pad_maximum_fusion.1), kind=kLoop, calls=%fused_computation.6 | loop fusion | flops 847872 | bytes 4557312 | tf_op jit(solution)/shard_map/mul | solution.py:58
  39.3 5.8 %mul.172 = f32[192,4416]{1,0:T(8,128)} reshape(f32[3,64,46,96]{3,2,1,0:T(8,128)} %broadcast_multiply_fusion) | data formatting | bytes 6782976 | tf_op jit(solution)/shard_map/mul | solution.py:58
  45.1 4.1 %reduce-precision_convert_fusion = (bf16[192,4416]{1,0:T(8,128)(2,1)}, bf16[192,4416]{1,0:T(8,128)(2,1)}) fusion(f32[192,4416]{1,0:T(8,128)} %mul.172), kind=kLoop, calls=%fused_computation.2 | loop fusion | flops 3391488 | bytes 6782976 | tf_op jit(solution)/shard_map/convert_element_type | solution.py:61
  49.2 0.0 copy-start.3
  49.2 4.0 %pad_maximum_fusion.weights_ref = bf16[384,4416]{1,0:T(8,128)(2,1)} fusion(bf16[192,4416]{1,0:T(8,128)(2,1)} %get-tuple-element.6, bf16[192,4416]{1,0:T(8,128)(2,1)} %get-tuple-element.5), kind=kLoop, calls=%fused_computation.4 | loop fusion | flops 6782976 | bytes 6782976 | tf_op jit(solution)/shard_map/concatenate | solution.py:61
  53.2 0.0 copy-done.3
  53.2 2.7 %convolution_convert_fusion = bf16[46,32768]{1,0:T(8,128)(2,1)} fusion(s32[32768]{0:T(1024)S(1)} %subtract_bitcast_fusion, bf16[45,21]{0,1:T(8,128)(2,1)S(1)} %copy-done.3), kind=kOutput, calls=%fused_computation | convolution fusion | flops 65503232 | bytes 3147618 | tf_op jit(solution)/shard_map/dot_general | solution.py:41
  55.9 0.3 fusion.21
  56.1 0.0 collective-permute-done.4
  56.1 0.0 collective-permute-done.5
  56.1 1.2 %concatenate.9 = bf16[64,2068]{1,0:T(8,128)(2,1)S(1)} concatenate(bf16[64,10]{1,0:T(8,128)(2,1)S(1)} %collective-permute-done.4, bf16[64,2048]{1,0:T(8,128)(2,1)} %param.10, bf16[64,10]{1,0:T(8,128)(2,1)S(1)} %collective-permute-done.5), dimensions={1} | concatenate | bytes 529408 | tf_op jit(solution)/shard_map/concatenate | solution.py:32
  57.4 10.0 %collective-permute-start.6 = (bf16[10,2068]{1,0:T(8,128)(2,1)S(1)}, bf16[10,2068]{1,0:T(8,128)(2,1)S(1)}, u32[]{:S(2)}, u32[]{:S(2)}) collective-permute-start(bf16[10,2068]{1,0:T(8,128)(2,1)S(1)} %get-tuple-element.11), channel_id=1, source_target_pairs={{0,1},{1,2},{2,3},{3,4},{4,5},{5,6},{6,7},{8,9},{9,10},{10,11},{11... | collective-permute-start | bytes 124088 | tf_op jit(solution)/shard_map/ppermute | solution.py:30
  67.4 1.3 %collective-permute-start.7 = (bf16[10,2068]{1,0:T(8,128)(2,1)S(1)}, bf16[10,2068]{1,0:T(8,128)(2,1)S(1)}, u32[]{:S(2)}, u32[]{:S(2)}) collective-permute-start(bf16[10,2068]{1,0:T(8,128)(2,1)S(1)} %get-tuple-element.12), channel_id=1, source_target_pairs={{1,0},{2,1},{3,2},{4,3},{5,4},{6,5},{7,6},{9,8},{10,9},{11,10},{12... | collective-permute-start | bytes 124088 | tf_op jit(solution)/shard_map/ppermute | solution.py:31
  68.7 0.6 pad_maximum_fusion.2.trig_ref
  69.3 2.7 %copy.8 = bf16[6,8,256,128]{3,2,1,0:T(8,128)(2,1)S(1)} copy(bf16[6,8,256,128]{3,1,2,0:T(8,128)(2,1)} %bitcast.24) | data formatting | bytes 6291456
  72.0 2.0 %slice.72.band_ref = bf16[46,256,128]{2,1,0:T(8,128)(2,1)} slice(bf16[48,256,128]{2,1,0:T(8,128)(2,1)S(1)} %bitcast.25), slice={[0:46], [0:256], [0:128]} | slice | bytes 6029312 | tf_op jit(solution)/shard_map/reshape | solution.py:42
  74.0 0.0 collective-permute-done.6
  74.0 2.0 %collective-permute-start.3 = (f32[64,2048]{1,0:T(8,128)}, f32[64,2048]{1,0:T(8,128)S(1)}, u32[]{:S(2)}, u32[]{:S(2)}) collective-permute-start(f32[64,2048]{1,0:T(8,128)} %get-tuple-element.8), channel_id=1, source_target_pairs={{0,16},{8,24},{16,32},{24,40},{32,48},{40,56},{48,64},{56,72},{64,... | collective-permute-start | bytes 1572872 | tf_op jit(solution)/shard_map/ppermute | solution.py:20
  76.0 5.5 %collective-permute-done.7 = bf16[10,2068]{1,0:T(8,128)(2,1)S(1)} collective-permute-done((bf16[10,2068]{1,0:T(8,128)(2,1)S(1)}, bf16[10,2068]{1,0:T(8,128)(2,1)S(1)}, u32[]{:S(2)}, u32[]{:S(2)}) %collective-permute-start.7) | collective-permute-done | bytes 41392 | tf_op jit(solution)/shard_map/ppermute | solution.py:31
  81.6 0.9 fusion.14.padded_ref
  82.4 23.1 %shard_map.73 = f32[64,2048]{1,0:T(8,128)} custom-call(bf16[96,2176]{1,0:T(8,128)(2,1)} %fusion.14.padded_ref, bf16[46,256,128]{2,1,0:T(8,128)(2,1)} %slice.72.band_ref, bf16[384,4416]{1,0:T(8,128)(2,1)} %pad_maximum_fusion.weights_ref, f32[2,2048]{1,0:T(2,128)} %pad_maximum_fusion.2.trig_ref), custom_call_target="tpu_custom_call" | custom-call | flops 11576279040 | bytes 8388608 | tf_op jit(solution)/shard_map/pallas_call | solution.py:108
  105.5 0.0 collective-permute-done
  105.5 0.0 collective-permute-done.1
  105.5 0.0 collective-permute-done.2
  105.5 0.0 collective-permute-done.3
  105.5 2.3 %fusion.9 = f32[64,2048]{1,0:T(8,128)} fusion(f32[64,2048]{1,0:T(8,128)} %shard_map.73, f32[64,2048]{1,0:T(8,128)S(1)} %collective-permute-done.3, f32[64,2048]{1,0:T(8,128)} %collective-permute-done.2, f32[64,2048]{1,0:T(8,128)S(1)} %collective-permute-done.1, f32[64,2048]{1,0:T(8,128)S(1)} %collective-permute-done, f32[320,2048]{1,0:T(8,128)} %copy-done.1), kind=kLoop, calls=%fused_computation.20 | loop fusion | flops 655360 | bytes 3670016 | tf_op jit(solution)/shard_map/sub | solution.py:152
  (7 shorter events, 0.1 us)
Async XLA Ops:
  0.0 13.0 %copy-start = (f32[256,2048]{1,0:T(8,128)S(1)}, f32[256,2048]{1,0:T(8,128)}, u32[]{:S(2)}) copy-start(f32[256,2048]{1,0:T(8,128)} %param.7) | copy-start | bytes 6291460
  1.0 55.2 %collective-permute-start.4 = (bf16[64,10]{1,0:T(8,128)(2,1)S(1)}, bf16[64,10]{1,0:T(8,128)(2,1)S(1)}, u32[]{:S(2)}, u32[]{:S(2)}) collective-permute-start(bf16[64,10]{1,0:T(8,128)(2,1)S(1)} %get-tuple-element.14), channel_id=1, source_target_pairs={{0,8},{8,16},{16,24},{24,32},{32,40},{40,48},{48,56},{56,64},{64,7... | collective-permute-start | bytes 3848 | tf_op jit(solution)/shard_map/ppermute | solution.py:30
  5.5 50.7 %collective-permute-start.5 = (bf16[64,10]{1,0:T(8,128)(2,1)S(1)}, bf16[64,10]{1,0:T(8,128)(2,1)S(1)}, u32[]{:S(2)}, u32[]{:S(2)}) collective-permute-start(bf16[64,10]{1,0:T(8,128)(2,1)S(1)} %get-tuple-element.13), channel_id=1, source_target_pairs={{8,0},{16,8},{24,16},{32,24},{40,32},{48,40},{56,48},{64,56},{72,6... | collective-permute-start | bytes 3848 | tf_op jit(solution)/shard_map/ppermute | solution.py:31
  14.5 1.5 %copy-start.1 = (f32[320,2048]{1,0:T(8,128)}, f32[320,2048]{1,0:T(8,128)S(1)}, u32[]{:S(2)}) copy-start(f32[320,2048]{1,0:T(8,128)S(1)} %fusion.16) | copy-start | bytes 7864324
  16.0 19.3 %copy-start.4 = (f32[45,6]{0,1:T(8,128)S(1)}, f32[45,6]{0,1:T(8,128)}, u32[]{:S(2)}) copy-start(f32[45,6]{0,1:T(8,128)} %param.13) | copy-start | bytes 3244
  16.0 19.3 %copy-start.2 = (bf16[45,21]{0,1:T(8,128)(2,1)S(1)}, bf16[45,21]{0,1:T(8,128)(2,1)}, u32[]{:S(2)}) copy-start(bf16[45,21]{0,1:T(8,128)(2,1)} %param.12) | copy-start | bytes 5674
  17.4 88.2 %collective-permute-start = (f32[64,2048]{1,0:T(8,128)}, f32[64,2048]{1,0:T(8,128)S(1)}, u32[]{:S(2)}, u32[]{:S(2)}) collective-permute-start(f32[64,2048]{1,0:T(8,128)} %get-tuple-element.7), channel_id=1, source_target_pairs={{0,496},{8,504},{16,0},{24,8},{32,16},{40,24},{48,32},{56,40},{64,... | collective-permute-start | bytes 1572872 | tf_op jit(solution)/shard_map/ppermute | solution.py:20
  29.3 76.2 %collective-permute-start.1 = (f32[64,2048]{1,0:T(8,128)}, f32[64,2048]{1,0:T(8,128)S(1)}, u32[]{:S(2)}, u32[]{:S(2)}) collective-permute-start(f32[64,2048]{1,0:T(8,128)} %get-tuple-element.10), channel_id=1, source_target_pairs={{0,504},{8,0},{16,8},{24,16},{32,24},{40,32},{48,40},{56,48},{64,5... | collective-permute-start | bytes 1572872 | tf_op jit(solution)/shard_map/ppermute | solution.py:20
  31.7 73.9 %collective-permute-start.2 = (f32[64,2048]{1,0:T(8,128)}, f32[64,2048]{1,0:T(8,128)}, u32[]{:S(2)}, u32[]{:S(2)}) collective-permute-start(f32[64,2048]{1,0:T(8,128)} %get-tuple-element.9), channel_id=1, source_target_pairs={{0,8},{8,16},{16,24},{24,32},{32,40},{40,48},{48,56},{56,64},{64,7... | collective-permute-start | bytes 1572872 | tf_op jit(solution)/shard_map/ppermute | solution.py:20
  49.2 4.0 %copy-start.3 = (bf16[45,21]{0,1:T(8,128)(2,1)S(1)}, bf16[45,21]{0,1:T(8,128)(2,1)}, u32[]{:S(2)}) copy-start(bf16[45,21]{0,1:T(8,128)(2,1)} %param.11) | copy-start | bytes 5674
  57.4 16.6 %collective-permute-start.6 = (bf16[10,2068]{1,0:T(8,128)(2,1)S(1)}, bf16[10,2068]{1,0:T(8,128)(2,1)S(1)}, u32[]{:S(2)}, u32[]{:S(2)}) collective-permute-start(bf16[10,2068]{1,0:T(8,128)(2,1)S(1)} %get-tuple-element.11), channel_id=1, source_target_pairs={{0,1},{1,2},{2,3},{3,4},{4,5},{5,6},{6,7},{8,9},{9,10},{10,11},{11... | collective-permute-start | bytes 124088 | tf_op jit(solution)/shard_map/ppermute | solution.py:30
  67.4 14.1 %collective-permute-start.7 = (bf16[10,2068]{1,0:T(8,128)(2,1)S(1)}, bf16[10,2068]{1,0:T(8,128)(2,1)S(1)}, u32[]{:S(2)}, u32[]{:S(2)}) collective-permute-start(bf16[10,2068]{1,0:T(8,128)(2,1)S(1)} %get-tuple-element.12), channel_id=1, source_target_pairs={{1,0},{2,1},{3,2},{4,3},{5,4},{6,5},{7,6},{9,8},{10,9},{11,10},{12... | collective-permute-start | bytes 124088 | tf_op jit(solution)/shard_map/ppermute | solution.py:31
  74.0 31.5 %collective-permute-start.3 = (f32[64,2048]{1,0:T(8,128)}, f32[64,2048]{1,0:T(8,128)S(1)}, u32[]{:S(2)}, u32[]{:S(2)}) collective-permute-start(f32[64,2048]{1,0:T(8,128)} %get-tuple-element.8), channel_id=1, source_target_pairs={{0,16},{8,24},{16,32},{24,40},{32,48},{40,56},{48,64},{56,72},{64,... | collective-permute-start | bytes 1572872 | tf_op jit(solution)/shard_map/ppermute | solution.py:20

commit v3 on v2

--- a/solution.py
+++ b/solution.py
@@ -13,6 +13,7 @@
 TILE = 128
 WIN = 256
 ROWS_PAD = 96
+BLOCK = 128
 
 
 def shifted(value, axis, by):
@@ -33,44 +34,45 @@
     return value
 
 
-def row_band(row_taps, n_basis):
-    taps = row_taps.shape[1]
-    offset = jnp.arange(WIN, dtype=jnp.int32)[:, None] - jnp.arange(TILE, dtype=jnp.int32)[None, :]
-    picks = (offset[None, :, :] == jnp.arange(taps, dtype=jnp.int32)[:, None, None]).astype(jnp.bfloat16)
-    padded_taps = jnp.pad(row_taps, ((0, n_basis - row_taps.shape[0]), (0, 0)))
-    band = jnp.dot(padded_taps, picks.reshape(taps, WIN * TILE), preferred_element_type=jnp.float32)
-    return band.astype(jnp.bfloat16).reshape(n_basis, WIN, TILE)
-
-
-def field_band(col_taps, coef, level, n_basis):
-    k_count, taps = col_taps.shape
-    p_rows = level.shape[0]
-    offset = jnp.arange(ROWS_PAD, dtype=jnp.int32)[None, :] - jnp.arange(p_rows, dtype=jnp.int32)[:, None]
-    picks = (offset[:, None, :] == jnp.arange(taps, dtype=jnp.int32)[None, :, None]).astype(jnp.float32)
-    taps_f = jnp.pad(col_taps.astype(jnp.float32), ((0, n_basis - k_count), (0, 0)))
-    shifted_taps = jnp.einsum("kp,ypr->ykr", taps_f, picks)
-    coef = jnp.pad(coef, ((0, n_basis - k_count), (0, 0)))
-    lv = level[:, None]
-    plain = coef[None, :, 0] + coef[None, :, 1] * lv + coef[None, :, 2] * (lv * lv)
-    with_cos = coef[None, :, 3] + coef[None, :, 5] * lv
-    with_sin = jnp.broadcast_to(coef[None, :, 4], plain.shape)
-    scale = jnp.stack([plain, with_cos, with_sin])
-    weights = (scale[:, :, :, None] * shifted_taps[None]).reshape(3 * p_rows, n_basis * ROWS_PAD)
-    high = lax.reduce_precision(weights, exponent_bits=8, mantissa_bits=7)
-    low = weights - high
-    return jnp.concatenate([high.astype(jnp.bfloat16), low.astype(jnp.bfloat16)], axis=0)
-
-
-def conv_kernel(n_tiles, n_basis, p_rows, padded_ref, band_ref, weights_ref, trig_ref, out_ref, rp_ref, windows_ref):
+def conv_kernel(n_tiles, n_basis, p_rows, coef_ref, utaps_ref, vtaps_ref, level_ref, trig_ref, padded_ref,
+                out_ref, rp_ref, windows_ref, weights_ref):
+    f32, bf16 = jnp.float32, jnp.bfloat16
     for t in range(n_tiles):
         windows_ref[t * ROWS_PAD:(t + 1) * ROWS_PAD, :] = padded_ref[:, t * TILE:t * TILE + WIN]
 
+    level = level_ref[...]
+    level_sq = level * level
+
+    def weight_step(k, carry):
+        vrow = jnp.broadcast_to(vtaps_ref[pl.ds(k, 1), :], (p_rows, BLOCK))
+        shifted_taps = pltpu.roll(vrow, 0, 1, stride=1, stride_axis=0)
+        plain = coef_ref[k, 0] + coef_ref[k, 1] * level + coef_ref[k, 2] * level_sq
+        with_cos = coef_ref[k, 3] + coef_ref[k, 5] * level
+        col = pl.multiple_of(k * BLOCK, BLOCK)
+        for term, scale in enumerate((plain, with_cos, coef_ref[k, 4])):
+            w = scale * shifted_taps
+            high = w.astype(bf16)
+            low = (w - high.astype(f32)).astype(bf16)
+            weights_ref[term * p_rows:(term + 1) * p_rows, pl.ds(col, BLOCK)] = high
+            weights_ref[(3 + term) * p_rows:(4 + term) * p_rows, pl.ds(col, BLOCK)] = low
+        rp_ref[pl.ds(k * BLOCK + ROWS_PAD, BLOCK - ROWS_PAD), :] = jnp.zeros(
+            (BLOCK - ROWS_PAD, rp_ref.shape[1]), bf16
+        )
+        return carry
+
+    lax.fori_loop(0, n_basis, weight_step, 0)
+
     def row_step(step, carry):
-        rhs = jnp.concatenate([band_ref[2 * step], band_ref[2 * step + 1]], axis=1)
-        part = jnp.dot(windows_ref[...], rhs, preferred_element_type=jnp.float32)
-        part = part.astype(jnp.bfloat16)
+        bands = []
         for half in range(2):
-            base = pl.multiple_of((2 * step + half) * ROWS_PAD, ROWS_PAD)
+            urow = jnp.broadcast_to(utaps_ref[pl.ds(2 * step + half, 1), :], (TILE, WIN))
+            bands.append(pltpu.roll(urow, 0, 1, stride=1, stride_axis=0))
+        band_t = jnp.concatenate(bands, axis=0).astype(bf16)
+        part = lax.dot_general(
+            windows_ref[...], band_t, (((1,), (1,)), ((), ())), preferred_element_type=f32
+        ).astype(bf16)
+        for half in range(2):
+            base = pl.multiple_of((2 * step + half) * BLOCK, BLOCK)
             for t in range(n_tiles):
                 rp_ref[pl.ds(base, ROWS_PAD), t * TILE:(t + 1) * TILE] = part[
                     t * ROWS_PAD:(t + 1) * ROWS_PAD, half * TILE:(half + 1) * TILE
@@ -83,7 +85,7 @@
 
     def col_step(step, carry):
         col = pl.multiple_of(step * chunk, chunk)
-        sums = jnp.dot(weights_ref[...], rp_ref[:, pl.ds(col, chunk)], preferred_element_type=jnp.float32)
+        sums = jnp.dot(weights_ref[...], rp_ref[:, pl.ds(col, chunk)], preferred_element_type=f32)
         lo = 3 * p_rows
         plain = sums[0:p_rows] + sums[lo:lo + p_rows]
         with_cos = sums[p_rows:2 * p_rows] + sums[lo + p_rows:lo + 2 * p_rows]
@@ -100,23 +102,28 @@
     p_rows = level.shape[0]
     width = trig.shape[1]
     n_tiles = width // TILE
-    n_basis = row_taps.shape[0] + (row_taps.shape[0] % 2)
+    k_count = row_taps.shape[0]
+    n_basis = k_count + (k_count % 2)
     padded = jnp.pad(padded, ((0, ROWS_PAD - padded.shape[0]), (0, n_tiles * TILE + WIN - TILE - padded.shape[1])))
-    band = row_band(row_taps, n_basis)
-    weights = field_band(col_taps, coef, level, n_basis)
-    flops = 2 * n_tiles * ROWS_PAD * WIN * n_basis * TILE + 2 * weights.shape[0] * weights.shape[1] * width
+    utaps = jnp.pad(row_taps.astype(jnp.float32), ((0, n_basis - k_count), (0, WIN - row_taps.shape[1])))
+    vtaps = jnp.pad(col_taps.astype(jnp.float32), ((0, n_basis - k_count), (0, BLOCK - col_taps.shape[1])))
+    coef = jnp.pad(coef, ((0, n_basis - k_count), (0, 0)))
+    level = jnp.broadcast_to(level[:, None], (p_rows, BLOCK))
+    flops = 2 * n_tiles * ROWS_PAD * WIN * n_basis * TILE + 2 * 6 * p_rows * n_basis * BLOCK * width
+    vmem = pl.BlockSpec(memory_space=pltpu.VMEM)
     return pl.pallas_call(
         functools.partial(conv_kernel, n_tiles, n_basis, p_rows),
         out_shape=jax.ShapeDtypeStruct((p_rows, width), jnp.float32),
-        in_specs=[pl.BlockSpec(memory_space=pltpu.VMEM)] * 4,
-        out_specs=pl.BlockSpec(memory_space=pltpu.VMEM),
+        in_specs=[pl.BlockSpec(memory_space=pltpu.SMEM)] + [vmem] * 5,
+        out_specs=vmem,
         scratch_shapes=[
-            pltpu.VMEM((n_basis * ROWS_PAD, width), jnp.bfloat16),
+            pltpu.VMEM((n_basis * BLOCK, width), jnp.bfloat16),
             pltpu.VMEM((n_tiles * ROWS_PAD, WIN), jnp.bfloat16),
+            pltpu.VMEM((6 * p_rows, n_basis * BLOCK), jnp.bfloat16),
         ],
         compiler_params=pltpu.CompilerParams(vmem_limit_bytes=60 * 1024 * 1024),
-        cost_estimate=pl.CostEstimate(flops=flops, transcendentals=0, bytes_accessed=8 * 1024 * 1024),
-    )(padded, band, weights, trig)
+        cost_estimate=pl.CostEstimate(flops=flops, transcendentals=0, bytes_accessed=4 * 1024 * 1024),
+    )(coef, utaps, vtaps, level, trig, padded)
 
 
 def local(exposure, slots, target_rows, template, row_taps, col_taps, coef):

time: 108 us -> 114 us (1.056)
  the two profiles are of different devices: /device:TPU:1 before, /device:TPU:24 now
where the time goes in v3:
time: 114 us; the launch traced here: 113 us
  starting transfers between devices  64 us (56%)
  Pallas kernels  29.7 us (26%)
  other arithmetic  7.58 us (7%)
  local copies, waits for them, and re-layouts  7.41 us (6%)
  waiting for transfers between devices  3.26 us (3%)
  matrix products  1.42 us (1%)
    ppermute x4, starting transfers between devices, shifted(): lax.ppermute(value, axis, [(i, (i + by) % length) for i in range(length)])  31.8 us
    pallas_call x1, Pallas kernels, matched_template(): pl.pallas_call(functools.partial(conv_kernel, n_tiles, n_basis, p_rows),...  29.7 us
    ppermute x2, starting transfers between devices, extended(): after = lax.ppermute(initial, axis, down)  22 us
    ppermute x2, starting transfers between devices, extended(): before = lax.ppermute(last, axis, up)  10.1 us
    ppermute x2, waiting for transfers between devices, extended(): before = lax.ppermute(last, axis, up)  3.24 us
    sub x1, other arithmetic, local(): return science - matched  2.33 us
  transfers between devices with their start and end apart: 8, of which 1 were waited for; matrix products, arithmetic and copies ran while one was open for 10% of the time, Pallas kernels for 26%

profile of v3, /device:TPU:24, one launch (start us, length us, event | category | flops | bytes accessed | tf_op | source)
XLA Modules:
  0.0 113.5 jit_solution(12501649383521929540)
XLA Ops:
  0.0 0.0 copy-start
  0.0 1.0 fusion.19
  1.0 14.8 %collective-permute-start.5 = (bf16[64,10]{1,0:T(8,128)(2,1)S(1)}, bf16[64,10]{1,0:T(8,128)(2,1)S(1)}, u32[]{:S(2)}, u32[]{:S(2)}) collective-permute-start(bf16[64,10]{1,0:T(8,128)(2,1)S(1)} %get-tuple-element.11), channel_id=1, source_target_pairs={{8,0},{16,8},{24,16},{32,24},{40,32},{48,40},{56,48},{64,56},{72,6... | collective-permute-start | bytes 3848 | tf_op jit(solution)/shard_map/ppermute | solution.py:32
  15.8 1.9 %collective-permute-start.4 = (bf16[64,10]{1,0:T(8,128)(2,1)S(1)}, bf16[64,10]{1,0:T(8,128)(2,1)S(1)}, u32[]{:S(2)}, u32[]{:S(2)}) collective-permute-start(bf16[64,10]{1,0:T(8,128)(2,1)S(1)} %get-tuple-element.12), channel_id=1, source_target_pairs={{0,8},{8,16},{16,24},{24,32},{32,40},{40,48},{48,56},{56,64},{64,7... | collective-permute-start | bytes 3848 | tf_op jit(solution)/shard_map/ppermute | solution.py:31
  17.7 0.7 broadcast_multiply_fusion
  18.4 0.7 add.82
  19.0 0.0 copy-done
  19.0 1.4 %fusion.13 = f32[320,2048]{1,0:T(8,128)S(1)} fusion(f32[256,2048]{1,0:T(8,128)S(1)} %copy-done, s32[256]{0:T(256)S(1)} %add.82), kind=kOutput, calls=%fused_computation.17 | convolution fusion | flops 2013347840 | bytes 4719616 | tf_op jit(solution)/shard_map/dot_general | solution.py:136
  20.5 0.0 copy-start.1
  20.5 1.5 %copy-done.1 = f32[320,2048]{1,0:T(8,128)} copy-done((f32[320,2048]{1,0:T(8,128)}, f32[320,2048]{1,0:T(8,128)S(1)}, u32[]{:S(2)}) %copy-start.1) | copy-done | bytes 2621464
  22.0 0.0 copy-start.2
  22.0 0.0 copy-start.3
  22.0 0.0 copy-start.4
  22.0 1.4 %fusion.17 = (f32[64,2048]{1,0:T(8,128)}, f32[64,2048]{1,0:T(8,128)}, f32[64,2048]{1,0:T(8,128)}, f32[64,2048]{1,0:T(8,128)}) fusion(f32[320,2048]{1,0:T(8,128)S(1)} %fusion.13), kind=kLoop, calls=%fused_computation.27 | loop fusion | bytes 4194304 | tf_op jit(solution)/shard_map/slice | solution.py:142
  23.4 3.0 %collective-permute-start = (f32[64,2048]{1,0:T(8,128)}, f32[64,2048]{1,0:T(8,128)S(1)}, u32[]{:S(2)}, u32[]{:S(2)}) collective-permute-start(f32[64,2048]{1,0:T(8,128)} %get-tuple-element.5), channel_id=1, source_target_pairs={{0,496},{8,504},{16,0},{24,8},{32,16},{40,24},{48,32},{56,40},{64,... | collective-permute-start | bytes 1572872 | tf_op jit(solution)/shard_map/ppermute | solution.py:21
  26.4 2.9 %collective-permute-start.3 = (f32[64,2048]{1,0:T(8,128)}, f32[64,2048]{1,0:T(8,128)S(1)}, u32[]{:S(2)}, u32[]{:S(2)}) collective-permute-start(f32[64,2048]{1,0:T(8,128)} %get-tuple-element.6), channel_id=1, source_target_pairs={{0,16},{8,24},{16,32},{24,40},{32,48},{40,56},{48,64},{56,72},{64,... | collective-permute-start | bytes 1572872 | tf_op jit(solution)/shard_map/ppermute | solution.py:21
  29.2 10.5 %collective-permute-start.2 = (f32[64,2048]{1,0:T(8,128)}, f32[64,2048]{1,0:T(8,128)}, u32[]{:S(2)}, u32[]{:S(2)}) collective-permute-start(f32[64,2048]{1,0:T(8,128)} %get-tuple-element.7), channel_id=1, source_target_pairs={{0,8},{8,16},{16,24},{24,32},{32,40},{40,48},{48,56},{56,64},{64,7... | collective-permute-start | bytes 1572872 | tf_op jit(solution)/shard_map/ppermute | solution.py:21
  39.7 0.0 copy-done.2
  39.7 0.1 copy.9
  39.8 0.0 copy-done.3
  39.8 0.1 copy.10
  40.0 0.3 fusion.15
  40.2 0.6 pad_convert_fusion.utaps_ref
  40.9 0.6 pad_maximum_fusion.trig_ref
  41.5 0.6 pad_convert_fusion.1.vtaps_ref
  42.1 0.0 collective-permute-done.5
  42.1 0.0 collective-permute-done.4
  42.1 1.2 %concatenate.6 = bf16[64,2068]{1,0:T(8,128)(2,1)S(1)} concatenate(bf16[64,10]{1,0:T(8,128)(2,1)S(1)} %collective-permute-done.4, bf16[64,2048]{1,0:T(8,128)(2,1)} %param.10, bf16[64,10]{1,0:T(8,128)(2,1)S(1)} %collective-permute-done.5), dimensions={1} | concatenate | bytes 529408 | tf_op jit(solution)/shard_map/concatenate | solution.py:33
  43.3 0.7 fusion.18
  44.0 8.2 %collective-permute-start.6 = (bf16[10,2068]{1,0:T(8,128)(2,1)}, bf16[10,2068]{1,0:T(8,128)(2,1)S(1)}, u32[]{:S(2)}, u32[]{:S(2)}) collective-permute-start(bf16[10,2068]{1,0:T(8,128)(2,1)} %get-tuple-element.9), channel_id=1, source_target_pairs={{0,1},{1,2},{2,3},{3,4},{4,5},{5,6},{6,7},{8,9},{9,10},{10,11},{11... | collective-permute-start | bytes 124088 | tf_op jit(solution)/shard_map/ppermute | solution.py:31
  52.2 7.2 %collective-permute-start.7 = (bf16[10,2068]{1,0:T(8,128)(2,1)}, bf16[10,2068]{1,0:T(8,128)(2,1)}, u32[]{:S(2)}, u32[]{:S(2)}) collective-permute-start(bf16[10,2068]{1,0:T(8,128)(2,1)} %get-tuple-element.10), channel_id=1, source_target_pairs={{1,0},{2,1},{3,2},{4,3},{5,4},{6,5},{7,6},{9,8},{10,9},{11,10},{12... | collective-permute-start | bytes 124088 | tf_op jit(solution)/shard_map/ppermute | solution.py:32
  59.4 0.0 copy-done.4
  59.4 0.1 copy.8
  59.5 0.6 pad.20.coef_ref
  60.2 3.2 %collective-permute-done.6 = bf16[10,2068]{1,0:T(8,128)(2,1)S(1)} collective-permute-done((bf16[10,2068]{1,0:T(8,128)(2,1)}, bf16[10,2068]{1,0:T(8,128)(2,1)S(1)}, u32[]{:S(2)}, u32[]{:S(2)}) %collective-permute-start.6) | collective-permute-done | bytes 41392 | tf_op jit(solution)/shard_map/ppermute | solution.py:31
  63.4 15.5 %collective-permute-start.1 = (f32[64,2048]{1,0:T(8,128)}, f32[64,2048]{1,0:T(8,128)S(1)}, u32[]{:S(2)}, u32[]{:S(2)}) collective-permute-start(f32[64,2048]{1,0:T(8,128)} %get-tuple-element.8), channel_id=1, source_target_pairs={{0,504},{8,0},{16,8},{24,16},{32,24},{40,32},{48,40},{56,48},{64,5... | collective-permute-start | bytes 1572872 | tf_op jit(solution)/shard_map/ppermute | solution.py:21
  79.0 0.0 collective-permute-done.7
  79.0 1.8 %fusion.12.padded_ref = bf16[96,2176]{1,0:T(8,128)(2,1)} fusion(bf16[10,2068]{1,0:T(8,128)(2,1)} %collective-permute-done.7, bf16[64,2068]{1,0:T(8,128)(2,1)S(1)} %concatenate.6, bf16[10,2068]{1,0:T(8,128)(2,1)S(1)} %collective-permute-done.6), kind=kLoop, calls=%fused_computation.15 | loop fusion | flops 3133440 | bytes 765216 | tf_op jit(solution)/shard_map/concatenate | solution.py:33
  80.8 0.7 broadcast_in_dim.2.level_ref
  81.4 29.7 %shard_map.73 = f32[64,2048]{1,0:T(8,128)} custom-call(f32[46,6]{1,0:T(8,128)} %pad.20.coef_ref, f32[46,256]{1,0:T(8,128)} %pad_convert_fusion.utaps_ref, f32[46,128]{1,0:T(8,128)} %pad_convert_fusion.1.vtaps_ref, f32[64,128]{1,0:T(8,128)} %broadcast_in_dim.2.level_ref, f32[2,2048]{1,0:T(2,128)} %pad_maximum_fusion.trig_ref, bf16[96,2176]{1,0:T(8,128)(2,1)} %fusion.12.padded_ref), custom_call_target="tpu_custom_call" | custom-call | flops 13891534848 | bytes 4194304 | tf_op jit(solution)/shard_map/pallas_call | solution.py:114
  111.1 0.0 collective-permute-done
  111.1 0.0 collective-permute-done.3
  111.1 0.0 collective-permute-done.2
  111.2 0.0 collective-permute-done.1
  111.2 2.3 %fusion.7 = f32[64,2048]{1,0:T(8,128)} fusion(f32[64,2048]{1,0:T(8,128)} %shard_map.73, f32[64,2048]{1,0:T(8,128)S(1)} %collective-permute-done.3, f32[64,2048]{1,0:T(8,128)} %collective-permute-done.2, f32[64,2048]{1,0:T(8,128)S(1)} %collective-permute-done.1, f32[64,2048]{1,0:T(8,128)S(1)} %collective-permute-done, f32[320,2048]{1,0:T(8,128)} %copy-done.1), kind=kLoop, calls=%fused_computation.10 | loop fusion | flops 655360 | bytes 3670016 | tf_op jit(solution)/shard_map/sub | solution.py:159
  (1 shorter events, 0.0 us)
Async XLA Ops:
  0.0 19.0 %copy-start = (f32[256,2048]{1,0:T(8,128)S(1)}, f32[256,2048]{1,0:T(8,128)}, u32[]{:S(2)}) copy-start(f32[256,2048]{1,0:T(8,128)} %param.7) | copy-start | bytes 6291460
  1.0 41.1 %collective-permute-start.5 = (bf16[64,10]{1,0:T(8,128)(2,1)S(1)}, bf16[64,10]{1,0:T(8,128)(2,1)S(1)}, u32[]{:S(2)}, u32[]{:S(2)}) collective-permute-start(bf16[64,10]{1,0:T(8,128)(2,1)S(1)} %get-tuple-element.11), channel_id=1, source_target_pairs={{8,0},{16,8},{24,16},{32,24},{40,32},{48,40},{56,48},{64,56},{72,6... | collective-permute-start | bytes 3848 | tf_op jit(solution)/shard_map/ppermute | solution.py:32
  15.8 26.3 %collective-permute-start.4 = (bf16[64,10]{1,0:T(8,128)(2,1)S(1)}, bf16[64,10]{1,0:T(8,128)(2,1)S(1)}, u32[]{:S(2)}, u32[]{:S(2)}) collective-permute-start(bf16[64,10]{1,0:T(8,128)(2,1)S(1)} %get-tuple-element.12), channel_id=1, source_target_pairs={{0,8},{8,16},{16,24},{24,32},{32,40},{40,48},{48,56},{56,64},{64,7... | collective-permute-start | bytes 3848 | tf_op jit(solution)/shard_map/ppermute | solution.py:31
  20.5 1.5 %copy-start.1 = (f32[320,2048]{1,0:T(8,128)}, f32[320,2048]{1,0:T(8,128)S(1)}, u32[]{:S(2)}) copy-start(f32[320,2048]{1,0:T(8,128)S(1)} %fusion.13) | copy-start | bytes 7864324
  22.0 17.7 %copy-start.2 = (bf16[45,21]{0,1:T(8,128)(2,1)S(1)}, bf16[45,21]{0,1:T(8,128)(2,1)}, u32[]{:S(2)}) copy-start(bf16[45,21]{0,1:T(8,128)(2,1)} %param.11) | copy-start | bytes 5674
  22.0 17.9 %copy-start.3 = (bf16[45,21]{0,1:T(8,128)(2,1)S(1)}, bf16[45,21]{0,1:T(8,128)(2,1)}, u32[]{:S(2)}) copy-start(bf16[45,21]{0,1:T(8,128)(2,1)} %param.12) | copy-start | bytes 5674
  22.0 37.5 %copy-start.4 = (f32[45,6]{0,1:T(8,128)S(1)}, f32[45,6]{0,1:T(8,128)}, u32[]{:S(2)}) copy-start(f32[45,6]{0,1:T(8,128)} %param.13) | copy-start | bytes 3244
  23.4 87.7 %collective-permute-start = (f32[64,2048]{1,0:T(8,128)}, f32[64,2048]{1,0:T(8,128)S(1)}, u32[]{:S(2)}, u32[]{:S(2)}) collective-permute-start(f32[64,2048]{1,0:T(8,128)} %get-tuple-element.5), channel_id=1, source_target_pairs={{0,496},{8,504},{16,0},{24,8},{32,16},{40,24},{48,32},{56,40},{64,... | collective-permute-start | bytes 1572872 | tf_op jit(solution)/shard_map/ppermute | solution.py:21
  26.4 84.8 %collective-permute-start.3 = (f32[64,2048]{1,0:T(8,128)}, f32[64,2048]{1,0:T(8,128)S(1)}, u32[]{:S(2)}, u32[]{:S(2)}) collective-permute-start(f32[64,2048]{1,0:T(8,128)} %get-tuple-element.6), channel_id=1, source_target_pairs={{0,16},{8,24},{16,32},{24,40},{32,48},{40,56},{48,64},{56,72},{64,... | collective-permute-start | bytes 1572872 | tf_op jit(solution)/shard_map/ppermute | solution.py:21
  29.2 81.9 %collective-permute-start.2 = (f32[64,2048]{1,0:T(8,128)}, f32[64,2048]{1,0:T(8,128)}, u32[]{:S(2)}, u32[]{:S(2)}) collective-permute-start(f32[64,2048]{1,0:T(8,128)} %get-tuple-element.7), channel_id=1, source_target_pairs={{0,8},{8,16},{16,24},{24,32},{32,40},{40,48},{48,56},{56,64},{64,7... | collective-permute-start | bytes 1572872 | tf_op jit(solution)/shard_map/ppermute | solution.py:21
  44.0 19.5 %collective-permute-start.6 = (bf16[10,2068]{1,0:T(8,128)(2,1)}, bf16[10,2068]{1,0:T(8,128)(2,1)S(1)}, u32[]{:S(2)}, u32[]{:S(2)}) collective-permute-start(bf16[10,2068]{1,0:T(8,128)(2,1)} %get-tuple-element.9), channel_id=1, source_target_pairs={{0,1},{1,2},{2,3},{3,4},{4,5},{5,6},{6,7},{8,9},{9,10},{10,11},{11... | collective-permute-start | bytes 124088 | tf_op jit(solution)/shard_map/ppermute | solution.py:31
  52.2 26.8 %collective-permute-start.7 = (bf16[10,2068]{1,0:T(8,128)(2,1)}, bf16[10,2068]{1,0:T(8,128)(2,1)}, u32[]{:S(2)}, u32[]{:S(2)}) collective-permute-start(bf16[10,2068]{1,0:T(8,128)(2,1)} %get-tuple-element.10), channel_id=1, source_target_pairs={{1,0},{2,1},{3,2},{4,3},{5,4},{6,5},{7,6},{9,8},{10,9},{11,10},{12... | collective-permute-start | bytes 124088 | tf_op jit(solution)/shard_map/ppermute | solution.py:32
  63.4 47.7 %collective-permute-start.1 = (f32[64,2048]{1,0:T(8,128)}, f32[64,2048]{1,0:T(8,128)S(1)}, u32[]{:S(2)}, u32[]{:S(2)}) collective-permute-start(f32[64,2048]{1,0:T(8,128)} %get-tuple-element.8), channel_id=1, source_target_pairs={{0,504},{8,0},{16,8},{24,16},{32,24},{40,32},{48,40},{56,48},{64,5... | collective-permute-start | bytes 1572872 | tf_op jit(solution)/shard_map/ppermute | solution.py:21

commit v4 on v3

--- a/solution.py
+++ b/solution.py
@@ -14,38 +14,74 @@
 WIN = 256
 ROWS_PAD = 96
 BLOCK = 128
-
-
-def shifted(value, axis, by):
-    length = lax.axis_size(axis)
-    return lax.ppermute(value, axis, [(i, (i + by) % length) for i in range(length)])
-
-
-def extended(value, sides, width, wrap):
-    for axis, dim in sides:
-        size, length = (lax.axis_size(axis), value.shape[dim])
-        up = [(i, (i + 1) % size) for i in range(size if wrap else size - 1)]
-        down = [(j, i) for i, j in up]
-        last = lax.slice_in_dim(value, length - width, length, axis=dim)
-        initial = lax.slice_in_dim(value, 0, width, axis=dim)
-        before = lax.ppermute(last, axis, up)
-        after = lax.ppermute(initial, axis, down)
-        value = jnp.concatenate([before, value, after], axis=dim)
-    return value
-
-
-def conv_kernel(n_tiles, n_basis, p_rows, coef_ref, utaps_ref, vtaps_ref, level_ref, trig_ref, padded_ref,
-                out_ref, rp_ref, windows_ref, weights_ref):
+EDGE = 16
+MESH = pl.DeviceIdType.MESH
+
+
+def conv_kernel(n_tiles, n_basis, p_rows, coef_ref, utaps_ref, vtaps_ref, level_ref, trig_ref, template_ref,
+                grid_ref, out_ref, rp_ref, windows_ref, weights_ref, ext_ref, arrived_ref,
+                halo_send, halo_recv, grid_send, grid_recv):
     f32, bf16 = jnp.float32, jnp.bfloat16
-    for t in range(n_tiles):
-        windows_ref[t * ROWS_PAD:(t + 1) * ROWS_PAD, :] = padded_ref[:, t * TILE:t * TILE + WIN]
+    n_ra, n_dec = lax.axis_size("ra"), lax.axis_size("dec")
+    ra, dec = lax.axis_index("ra"), lax.axis_index("dec")
+
+    def peer(d_ra, d_dec):
+        return (lax.rem(ra + d_ra + n_ra, n_ra), lax.rem(dec + d_dec + n_dec, n_dec))
+
+    width = template_ref.shape[1]
+    ext_ref[EDGE:EDGE + p_rows, TILE:TILE + width] = template_ref[...]
+    partners = [(1, 0), (-1, 0), (2, 0), (-2, 0), (0, 1), (0, -1), (1, 1), (1, -1), (-1, 1), (-1, -1)]
+    barrier = pltpu.get_barrier_semaphore()
+    for d_ra, d_dec in partners:
+        pl.semaphore_signal(barrier, inc=1, device_id=peer(d_ra, d_dec), device_id_type=MESH)
+    pl.semaphore_wait(barrier, len(partners))
+
+    top, bottom = slice(p_rows - EDGE, p_rows), slice(0, EDGE)
+    left, right = slice(width - TILE, width), slice(0, TILE)
+    all_rows, all_cols = slice(0, p_rows), slice(0, width)
+    inner_rows, inner_cols = slice(EDGE, EDGE + p_rows), slice(TILE, TILE + width)
+    low_rows, high_cols = slice(EDGE + p_rows, 2 * EDGE + p_rows), slice(TILE + width, 2 * TILE + width)
+    pieces = [
+        ((-1, 0), all_rows, left, inner_rows, slice(0, TILE)),
+        ((1, 0), all_rows, right, inner_rows, high_cols),
+        ((0, -1), top, all_cols, slice(0, EDGE), inner_cols),
+        ((0, 1), bottom, all_cols, low_rows, inner_cols),
+        ((-1, -1), top, left, slice(0, EDGE), slice(0, TILE)),
+        ((1, -1), top, right, slice(0, EDGE), high_cols),
+        ((-1, 1), bottom, left, low_rows, slice(0, TILE)),
+        ((1, 1), bottom, right, low_rows, high_cols),
+    ]
+    halo_copies = []
+    for n, ((s_ra, s_dec), my_rows, my_cols, rows, cols) in enumerate(pieces):
+        copy = pltpu.make_async_remote_copy(
+            src_ref=template_ref.at[my_rows, my_cols],
+            dst_ref=ext_ref.at[rows, cols],
+            send_sem=halo_send.at[n],
+            recv_sem=halo_recv.at[n],
+            device_id=peer(-s_ra, -s_dec),
+            device_id_type=MESH,
+        )
+        copy.start()
+        halo_copies.append(copy)
+    grid_copies = []
+    for m, slot in enumerate([s for s in range(2 * SPAN + 1) if s != SPAN]):
+        copy = pltpu.make_async_remote_copy(
+            src_ref=grid_ref.at[slot],
+            dst_ref=arrived_ref.at[m],
+            send_sem=grid_send.at[m],
+            recv_sem=grid_recv.at[m],
+            device_id=peer(slot - SPAN, 0),
+            device_id_type=MESH,
+        )
+        copy.start()
+        grid_copies.append(copy)
 
     level = level_ref[...]
     level_sq = level * level
 
     def weight_step(k, carry):
         vrow = jnp.broadcast_to(vtaps_ref[pl.ds(k, 1), :], (p_rows, BLOCK))
-        shifted_taps = pltpu.roll(vrow, 0, 1, stride=1, stride_axis=0)
+        shifted_taps = pltpu.roll(vrow, EDGE - HALF, 1, stride=1, stride_axis=0)
         plain = coef_ref[k, 0] + coef_ref[k, 1] * level + coef_ref[k, 2] * level_sq
         with_cos = coef_ref[k, 3] + coef_ref[k, 5] * level
         col = pl.multiple_of(k * BLOCK, BLOCK)
@@ -61,6 +97,19 @@
         return carry
 
     lax.fori_loop(0, n_basis, weight_step, 0)
+
+    for copy in halo_copies:
+        copy.wait()
+    keep_top = dec > 0
+    keep_bottom = dec < n_dec - 1
+    ext_ref[0:EDGE, :] = jnp.where(keep_top, ext_ref[0:EDGE, :], jnp.zeros_like(ext_ref[0:EDGE, :]))
+    ext_ref[EDGE + p_rows:, :] = jnp.where(
+        keep_bottom, ext_ref[EDGE + p_rows:, :], jnp.zeros_like(ext_ref[EDGE + p_rows:, :])
+    )
+    for t in range(n_tiles):
+        slab = ext_ref[:, t * TILE:t * TILE + 3 * TILE].astype(f32)
+        slab = pltpu.roll(slab, 3 * TILE - (TILE - HALF), 1)
+        windows_ref[t * ROWS_PAD:(t + 1) * ROWS_PAD, :] = slab[:, 0:WIN].astype(bf16)
 
     def row_step(step, carry):
         bands = []
@@ -97,33 +146,48 @@
 
     lax.fori_loop(0, out_ref.shape[1] // chunk, col_step, 0)
 
-
-def matched_template(padded, row_taps, col_taps, coef, level, trig):
+    for copy in grid_copies:
+        copy.wait()
+    science = grid_ref[SPAN]
+    for m in range(len(grid_copies)):
+        science = science + arrived_ref[m]
+    out_ref[...] = science - out_ref[...]
+
+
+def difference_image(template, grid, row_taps, col_taps, coef, level, trig):
     p_rows = level.shape[0]
     width = trig.shape[1]
     n_tiles = width // TILE
     k_count = row_taps.shape[0]
     n_basis = k_count + (k_count % 2)
-    padded = jnp.pad(padded, ((0, ROWS_PAD - padded.shape[0]), (0, n_tiles * TILE + WIN - TILE - padded.shape[1])))
     utaps = jnp.pad(row_taps.astype(jnp.float32), ((0, n_basis - k_count), (0, WIN - row_taps.shape[1])))
     vtaps = jnp.pad(col_taps.astype(jnp.float32), ((0, n_basis - k_count), (0, BLOCK - col_taps.shape[1])))
     coef = jnp.pad(coef, ((0, n_basis - k_count), (0, 0)))
     level = jnp.broadcast_to(level[:, None], (p_rows, BLOCK))
     flops = 2 * n_tiles * ROWS_PAD * WIN * n_basis * TILE + 2 * 6 * p_rows * n_basis * BLOCK * width
     vmem = pl.BlockSpec(memory_space=pltpu.VMEM)
+    n_out = 2 * SPAN
     return pl.pallas_call(
         functools.partial(conv_kernel, n_tiles, n_basis, p_rows),
         out_shape=jax.ShapeDtypeStruct((p_rows, width), jnp.float32),
-        in_specs=[pl.BlockSpec(memory_space=pltpu.SMEM)] + [vmem] * 5,
+        in_specs=[pl.BlockSpec(memory_space=pltpu.SMEM)] + [vmem] * 6,
         out_specs=vmem,
         scratch_shapes=[
             pltpu.VMEM((n_basis * BLOCK, width), jnp.bfloat16),
             pltpu.VMEM((n_tiles * ROWS_PAD, WIN), jnp.bfloat16),
             pltpu.VMEM((6 * p_rows, n_basis * BLOCK), jnp.bfloat16),
+            pltpu.VMEM((p_rows + 2 * EDGE, width + 2 * TILE), jnp.bfloat16),
+            pltpu.VMEM((n_out, p_rows, width), jnp.float32),
+            pltpu.SemaphoreType.DMA((8,)),
+            pltpu.SemaphoreType.DMA((8,)),
+            pltpu.SemaphoreType.DMA((n_out,)),
+            pltpu.SemaphoreType.DMA((n_out,)),
         ],
-        compiler_params=pltpu.CompilerParams(vmem_limit_bytes=60 * 1024 * 1024),
-        cost_estimate=pl.CostEstimate(flops=flops, transcendentals=0, bytes_accessed=4 * 1024 * 1024),
-    )(coef, utaps, vtaps, level, trig, padded)
+        compiler_params=pltpu.CompilerParams(
+            vmem_limit_bytes=60 * 1024 * 1024, collective_id=0, has_side_effects=True
+        ),
+        cost_estimate=pl.CostEstimate(flops=flops, transcendentals=0, bytes_accessed=8 * 1024 * 1024),
+    )(coef, utaps, vtaps, level, trig, template, grid)
 
 
 def local(exposure, slots, target_rows, template, row_taps, col_taps, coef):
@@ -136,14 +200,6 @@
     partial = jnp.dot(
         select, exposure, precision=lax.Precision.HIGHEST, preferred_element_type=jnp.float32
     ).reshape(n_slots, p_rows, width)
-    arrived = [partial[SPAN]]
-    for offset in range(-SPAN, SPAN + 1):
-        if offset != 0:
-            arrived.append(shifted(partial[SPAN + offset], "ra", offset))
-
-    widened = extended(template, (("ra", 1),), HALF, True)
-    padded = extended(widened, (("dec", 0),), HALF, False)
-
     total_rows = p_rows * lax.axis_size("dec")
     total_cols = width * lax.axis_size("ra")
     rows_y = lax.axis_index("dec") * p_rows + jnp.arange(p_rows, dtype=jnp.int32)
@@ -152,11 +208,7 @@
     phase = (2 * cols_x + 1).astype(jnp.float32) * (math.pi / total_cols)
     trig = jnp.stack([jnp.cos(phase), jnp.sin(phase)])
 
-    matched = matched_template(padded, row_taps, col_taps, coef, level, trig)
-    science = arrived[0]
-    for part in arrived[1:]:
-        science = science + part
-    return science - matched
+    return difference_image(template, partial, row_taps, col_taps, coef, level, trig)
 
 
 def solution(mesh):

time: 114 us -> 84.7 us (0.74)
  the two profiles are of different devices: /device:TPU:24 before, /device:TPU:64 now
where the time goes in v4:
time: 84.7 us; the launch traced here: 84.3 us
  Pallas kernels  72.3 us (85%)
  local copies, waits for them, and re-layouts  5.53 us (7%)
  other arithmetic  3.62 us (4%)
  matrix products  2.88 us (3%)
    pallas_call x1, Pallas kernels, difference_image(): pl.pallas_call(functools.partial(conv_kernel, n_tiles, n_basis, p_rows),...  72.3 us
    unnamed x6, local copies, waits for them, and re-layouts  4.25 us
    dot_general x1, matrix products, local(): jnp.dot(select, exposure, precision=lax.Precision.HIGHEST, preferred_elem...  2.88 us

profile of v4, /device:TPU:64, one launch (start us, length us, event | category | flops | bytes accessed | tf_op | source)
XLA Modules:
  0.0 84.3 jit_solution(13991275751052452871)
XLA Ops:
  0.0 0.0 copy-start
  0.0 0.8 broadcast_multiply_fusion
  0.8 0.7 add.76
  1.5 0.8 copy.9
  2.3 0.8 copy.10
  3.1 0.6 pad_convert_fusion.1.vtaps_ref
  3.7 0.3 fusion.2
  4.0 0.6 pad_maximum_fusion.trig_ref
  4.6 0.8 copy.8
  5.4 0.6 pad.16.coef_ref
  6.0 0.7 broadcast_in_dim.2.level_ref
  6.7 0.6 pad_convert_fusion.utaps_ref
  7.3 0.0 copy-done
  7.3 2.9 %fusion = f32[320,2048]{1,0:T(8,128)} fusion(f32[256,2048]{1,0:T(8,128)S(1)} %copy-done, s32[256]{0:T(256)S(1)} %add.76), kind=kOutput, calls=%fused_computation.1 | convolution fusion | flops 2013347840 | bytes 4719616 | tf_op jit(solution)/shard_map/dot_general | solution.py:200
  10.2 72.3 %shard_map.73 = f32[64,2048]{1,0:T(8,128)} custom-call(f32[46,6]{1,0:T(8,128)} %pad.16.coef_ref, f32[46,256]{1,0:T(8,128)} %pad_convert_fusion.utaps_ref, f32[46,128]{1,0:T(8,128)} %pad_convert_fusion.1.vtaps_ref, f32[64,128]{1,0:T(8,128)} %broadcast_in_dim.2.level_ref, f32[2,2048]{1,0:T(2,128)} %pad_maximum_fusion.trig_ref, bf16[64,2048]{1,0:T(8,128)(2,1)} %template_ref.1, ...), custom_call_target="tpu_custom_call" | custom-call | flops 13891534848 | bytes 8388608 | tf_op jit(solution)/shard_map/pallas_call | solution.py:170
  82.5 1.9 %copy.12 = f32[64,2048]{1,0:T(8,128)} copy(f32[64,2048]{1,0:T(8,128)} %shard_map.73) | data formatting | bytes 1048576
  (1 shorter events, 0.0 us)
Async XLA Ops:
  0.0 7.3 %copy-start = (f32[256,2048]{1,0:T(8,128)S(1)}, f32[256,2048]{1,0:T(8,128)}, u32[]{:S(2)}) copy-start(f32[256,2048]{1,0:T(8,128)} %param.7) | copy-start | bytes 6291460

commit v5 on v4

--- a/solution.py
+++ b/solution.py
@@ -16,10 +16,11 @@
 BLOCK = 128
 EDGE = 16
 MESH = pl.DeviceIdType.MESH
+OWN, MIXED, NEAR, FAR = range(4)
 
 
 def conv_kernel(n_tiles, n_basis, p_rows, coef_ref, utaps_ref, vtaps_ref, level_ref, trig_ref, template_ref,
-                grid_ref, out_ref, rp_ref, windows_ref, weights_ref, ext_ref, arrived_ref,
+                grid_ref, out_ref, rp_ref, windows_ref, weights_ref, ext_ref, arrived_ref, combined_ref,
                 halo_send, halo_recv, grid_send, grid_recv):
     f32, bf16 = jnp.float32, jnp.bfloat16
     n_ra, n_dec = lax.axis_size("ra"), lax.axis_size("dec")
@@ -63,18 +64,24 @@
         )
         copy.start()
         halo_copies.append(copy)
-    grid_copies = []
-    for m, slot in enumerate([s for s in range(2 * SPAN + 1) if s != SPAN]):
-        copy = pltpu.make_async_remote_copy(
-            src_ref=grid_ref.at[slot],
-            dst_ref=arrived_ref.at[m],
-            send_sem=grid_send.at[m],
-            recv_sem=grid_recv.at[m],
-            device_id=peer(slot - SPAN, 0),
+    sign = 2 * lax.rem(ra, 2) - 1
+
+    def grid_copy(src, slot, d_ra):
+        return pltpu.make_async_remote_copy(
+            src_ref=src,
+            dst_ref=arrived_ref.at[slot],
+            send_sem=grid_send.at[slot],
+            recv_sem=grid_recv.at[slot],
+            device_id=peer(d_ra, 0),
             device_id_type=MESH,
         )
+
+    to_partner = grid_copy(grid_ref.at[SPAN - sign], OWN, -sign)
+    to_combine = grid_copy(grid_ref.at[SPAN - 2 * sign], MIXED, -sign)
+    far = grid_copy(grid_ref.at[SPAN + 2 * sign], FAR, 2 * sign)
+    near = grid_copy(combined_ref, NEAR, sign)
+    for copy in (to_partner, to_combine, far):
         copy.start()
-        grid_copies.append(copy)
 
     level = level_ref[...]
     level_sq = level * level
@@ -100,6 +107,9 @@
 
     for copy in halo_copies:
         copy.wait()
+    to_combine.wait_recv()
+    combined_ref[...] = grid_ref[SPAN + sign] + arrived_ref[MIXED]
+    near.start()
     keep_top = dec > 0
     keep_bottom = dec < n_dec - 1
     ext_ref[0:EDGE, :] = jnp.where(keep_top, ext_ref[0:EDGE, :], jnp.zeros_like(ext_ref[0:EDGE, :]))
@@ -146,11 +156,11 @@
 
     lax.fori_loop(0, out_ref.shape[1] // chunk, col_step, 0)
 
-    for copy in grid_copies:
-        copy.wait()
-    science = grid_ref[SPAN]
-    for m in range(len(grid_copies)):
-        science = science + arrived_ref[m]
+    to_partner.wait()
+    to_combine.wait_send()
+    far.wait()
+    near.wait()
+    science = grid_ref[SPAN] + arrived_ref[OWN] + arrived_ref[NEAR] + arrived_ref[FAR]
     out_ref[...] = science - out_ref[...]
 
 
@@ -178,6 +188,7 @@
             pltpu.VMEM((6 * p_rows, n_basis * BLOCK), jnp.bfloat16),
             pltpu.VMEM((p_rows + 2 * EDGE, width + 2 * TILE), jnp.bfloat16),
             pltpu.VMEM((n_out, p_rows, width), jnp.float32),
+            pltpu.VMEM((p_rows, width), jnp.float32),
             pltpu.SemaphoreType.DMA((8,)),
             pltpu.SemaphoreType.DMA((8,)),
             pltpu.SemaphoreType.DMA((n_out,)),

time: 84.7 us -> 78.1 us (0.922)
  the two profiles are of different devices: /device:TPU:64 before, /device:TPU:321 now
where the time goes in v5:
time: 78.1 us; the launch traced here: 77.8 us
  Pallas kernels  65.7 us (84%)
  local copies, waits for them, and re-layouts  5.53 us (7%)
  other arithmetic  3.62 us (5%)
  matrix products  2.88 us (4%)
    pallas_call x1, Pallas kernels, difference_image(): pl.pallas_call(functools.partial(conv_kernel, n_tiles, n_basis, p_rows),...  65.7 us
    unnamed x6, local copies, waits for them, and re-layouts  4.25 us
    dot_general x1, matrix products, local(): jnp.dot(select, exposure, precision=lax.Precision.HIGHEST, preferred_elem...  2.88 us

profile of v5, /device:TPU:321, one launch (start us, length us, event | category | flops | bytes accessed | tf_op | source)
XLA Modules:
  0.0 77.8 jit_solution(8246633820665895178)
XLA Ops:
  0.0 0.0 copy-start
  0.0 0.8 %broadcast_multiply_fusion = s32[256,1]{0,1:T(1,128)S(1)} fusion(s32[256,1]{0,1:T(1,128)} %param.8), kind=kLoop, calls=%fused_computation.9 | loop fusion | flops 256 | bytes 2048 | tf_op jit(solution)/shard_map/mul | solution.py:209
  0.8 0.7 add.76
  1.5 0.8 %copy.9 = bf16[45,21]{1,0:T(8,128)(2,1)S(1)} copy(bf16[45,21]{0,1:T(8,128)(2,1)} %param.11) | data formatting | bytes 3780 | tf_op args[4]
  2.3 0.8 %copy.10 = bf16[45,21]{1,0:T(8,128)(2,1)S(1)} copy(bf16[45,21]{0,1:T(8,128)(2,1)} %param.12) | data formatting | bytes 3780 | tf_op args[5]
  3.1 0.6 pad_convert_fusion.1.vtaps_ref
  3.7 0.3 fusion.2
  4.0 0.6 pad_maximum_fusion.trig_ref
  4.6 0.8 %copy.8 = f32[45,6]{1,0:T(8,128)S(1)} copy(f32[45,6]{0,1:T(8,128)} %param.13) | data formatting | bytes 2160 | tf_op args[6]
  5.4 0.6 pad.16.coef_ref
  6.0 0.7 broadcast_in_dim.2.level_ref
  6.7 0.6 pad_convert_fusion.utaps_ref
  7.3 0.0 copy-done
  7.3 2.9 %fusion = f32[320,2048]{1,0:T(8,128)} fusion(f32[256,2048]{1,0:T(8,128)S(1)} %copy-done, s32[256]{0:T(256)S(1)} %add.76), kind=kOutput, calls=%fused_computation.1 | convolution fusion | flops 2013347840 | bytes 4719616 | tf_op jit(solution)/shard_map/dot_general | solution.py:211
  10.2 65.7 %shard_map.73 = f32[64,2048]{1,0:T(8,128)} custom-call(f32[46,6]{1,0:T(8,128)} %pad.16.coef_ref, f32[46,256]{1,0:T(8,128)} %pad_convert_fusion.utaps_ref, f32[46,128]{1,0:T(8,128)} %pad_convert_fusion.1.vtaps_ref, f32[64,128]{1,0:T(8,128)} %broadcast_in_dim.2.level_ref, f32[2,2048]{1,0:T(2,128)} %pad_maximum_fusion.trig_ref, bf16[64,2048]{1,0:T(8,128)(2,1)} %template_ref.1, ...), custom_call_target="tpu_custom_call" | custom-call | flops 13891534848 | bytes 8388608 | tf_op jit(solution)/shard_map/pallas_call | solution.py:180
  75.9 1.9 %copy.12 = f32[64,2048]{1,0:T(8,128)} copy(f32[64,2048]{1,0:T(8,128)} %shard_map.73) | data formatting | bytes 1048576
  (1 shorter events, 0.0 us)
Async XLA Ops:
  0.0 7.3 %copy-start = (f32[256,2048]{1,0:T(8,128)S(1)}, f32[256,2048]{1,0:T(8,128)}, u32[]{:S(2)}) copy-start(f32[256,2048]{1,0:T(8,128)} %param.7) | copy-start | bytes 6291460

commit v6 on v5

--- a/solution.py
+++ b/solution.py
@@ -19,7 +19,37 @@
 OWN, MIXED, NEAR, FAR = range(4)
 
 
-def conv_kernel(n_tiles, n_basis, p_rows, coef_ref, utaps_ref, vtaps_ref, level_ref, trig_ref, template_ref,
+def build_weights(coef_ref, vtaps_ref, weights_ref, rp_ref, n_basis, p_rows):
+    f32, bf16 = jnp.float32, jnp.bfloat16
+    rows = lax.axis_index("dec") * p_rows + lax.broadcasted_iota(jnp.int32, (p_rows, BLOCK), 0)
+    level = (2 * rows + 1).astype(f32) / (p_rows * lax.axis_size("dec")) - 1.0
+    level_sq = level * level
+
+    def weight_step(k, carry):
+        vrow = jnp.broadcast_to(vtaps_ref[pl.ds(k, 1), :], (p_rows, BLOCK))
+        shifted_taps = pltpu.roll(vrow, EDGE - HALF, 1, stride=1, stride_axis=0)
+        plain = coef_ref[k, 0] + coef_ref[k, 1] * level + coef_ref[k, 2] * level_sq
+        with_cos = coef_ref[k, 3] + coef_ref[k, 5] * level
+        col = pl.multiple_of(k * BLOCK, BLOCK)
+        for term, scale in enumerate((plain, with_cos, coef_ref[k, 4])):
+            w = scale * shifted_taps
+            high = w.astype(bf16)
+            low = (w - high.astype(f32)).astype(bf16)
+            weights_ref[term * p_rows:(term + 1) * p_rows, pl.ds(col, BLOCK)] = high
+            weights_ref[(3 + term) * p_rows:(4 + term) * p_rows, pl.ds(col, BLOCK)] = low
+        rp_ref[pl.ds(k * BLOCK + ROWS_PAD, BLOCK - ROWS_PAD), :] = jnp.zeros(
+            (BLOCK - ROWS_PAD, rp_ref.shape[1]), bf16
+        )
+        return carry
+
+    k_count = coef_ref.shape[0]
+    lax.fori_loop(0, k_count, weight_step, 0)
+    for k in range(k_count, n_basis):
+        weights_ref[:, k * BLOCK:(k + 1) * BLOCK] = jnp.zeros((weights_ref.shape[0], BLOCK), bf16)
+        rp_ref[k * BLOCK + ROWS_PAD:(k + 1) * BLOCK, :] = jnp.zeros((BLOCK - ROWS_PAD, rp_ref.shape[1]), bf16)
+
+
+def conv_kernel(n_tiles, n_basis, p_rows, coef_ref, utaps_ref, vtaps_ref, template_ref,
                 grid_ref, out_ref, rp_ref, windows_ref, weights_ref, ext_ref, arrived_ref, combined_ref,
                 halo_send, halo_recv, grid_send, grid_recv):
     f32, bf16 = jnp.float32, jnp.bfloat16
@@ -35,6 +65,8 @@
     barrier = pltpu.get_barrier_semaphore()
     for d_ra, d_dec in partners:
         pl.semaphore_signal(barrier, inc=1, device_id=peer(d_ra, d_dec), device_id_type=MESH)
+
+    build_weights(coef_ref, vtaps_ref, weights_ref, rp_ref, n_basis, p_rows)
     pl.semaphore_wait(barrier, len(partners))
 
     top, bottom = slice(p_rows - EDGE, p_rows), slice(0, EDGE)
@@ -83,33 +115,11 @@
     for copy in (to_partner, to_combine, far):
         copy.start()
 
-    level = level_ref[...]
-    level_sq = level * level
-
-    def weight_step(k, carry):
-        vrow = jnp.broadcast_to(vtaps_ref[pl.ds(k, 1), :], (p_rows, BLOCK))
-        shifted_taps = pltpu.roll(vrow, EDGE - HALF, 1, stride=1, stride_axis=0)
-        plain = coef_ref[k, 0] + coef_ref[k, 1] * level + coef_ref[k, 2] * level_sq
-        with_cos = coef_ref[k, 3] + coef_ref[k, 5] * level
-        col = pl.multiple_of(k * BLOCK, BLOCK)
-        for term, scale in enumerate((plain, with_cos, coef_ref[k, 4])):
-            w = scale * shifted_taps
-            high = w.astype(bf16)
-            low = (w - high.astype(f32)).astype(bf16)
-            weights_ref[term * p_rows:(term + 1) * p_rows, pl.ds(col, BLOCK)] = high
-            weights_ref[(3 + term) * p_rows:(4 + term) * p_rows, pl.ds(col, BLOCK)] = low
-        rp_ref[pl.ds(k * BLOCK + ROWS_PAD, BLOCK - ROWS_PAD), :] = jnp.zeros(
-            (BLOCK - ROWS_PAD, rp_ref.shape[1]), bf16
-        )
-        return carry
-
-    lax.fori_loop(0, n_basis, weight_step, 0)
-
-    for copy in halo_copies:
-        copy.wait()
     to_combine.wait_recv()
     combined_ref[...] = grid_ref[SPAN + sign] + arrived_ref[MIXED]
     near.start()
+    for copy in halo_copies:
+        copy.wait()
     keep_top = dec > 0
     keep_bottom = dec < n_dec - 1
     ext_ref[0:EDGE, :] = jnp.where(keep_top, ext_ref[0:EDGE, :], jnp.zeros_like(ext_ref[0:EDGE, :]))
@@ -149,8 +159,10 @@
         plain = sums[0:p_rows] + sums[lo:lo + p_rows]
         with_cos = sums[p_rows:2 * p_rows] + sums[lo + p_rows:lo + 2 * p_rows]
         with_sin = sums[2 * p_rows:3 * p_rows] + sums[lo + 2 * p_rows:lo + 3 * p_rows]
-        cosine = trig_ref[0:1, pl.ds(col, chunk)]
-        sine = trig_ref[1:2, pl.ds(col, chunk)]
+        cols = ra * width + col + lax.broadcasted_iota(jnp.int32, (1, chunk), 1)
+        phase = (2 * cols + 1).astype(f32) * (math.pi / (width * n_ra))
+        cosine = jnp.cos(phase)
+        sine = jnp.sin(phase)
         out_ref[:, pl.ds(col, chunk)] = plain + cosine * with_cos + sine * with_sin
         return carry
 
@@ -164,23 +176,20 @@
     out_ref[...] = science - out_ref[...]
 
 
-def difference_image(template, grid, row_taps, col_taps, coef, level, trig):
-    p_rows = level.shape[0]
-    width = trig.shape[1]
+def difference_image(template, grid, row_taps, col_taps, coef):
+    p_rows, width = template.shape
     n_tiles = width // TILE
     k_count = row_taps.shape[0]
     n_basis = k_count + (k_count % 2)
     utaps = jnp.pad(row_taps.astype(jnp.float32), ((0, n_basis - k_count), (0, WIN - row_taps.shape[1])))
     vtaps = jnp.pad(col_taps.astype(jnp.float32), ((0, n_basis - k_count), (0, BLOCK - col_taps.shape[1])))
-    coef = jnp.pad(coef, ((0, n_basis - k_count), (0, 0)))
-    level = jnp.broadcast_to(level[:, None], (p_rows, BLOCK))
     flops = 2 * n_tiles * ROWS_PAD * WIN * n_basis * TILE + 2 * 6 * p_rows * n_basis * BLOCK * width
     vmem = pl.BlockSpec(memory_space=pltpu.VMEM)
     n_out = 2 * SPAN
     return pl.pallas_call(
         functools.partial(conv_kernel, n_tiles, n_basis, p_rows),
         out_shape=jax.ShapeDtypeStruct((p_rows, width), jnp.float32),
-        in_specs=[pl.BlockSpec(memory_space=pltpu.SMEM)] + [vmem] * 6,
+        in_specs=[pl.BlockSpec(memory_space=pltpu.SMEM)] + [vmem] * 4,
         out_specs=vmem,
         scratch_shapes=[
             pltpu.VMEM((n_basis * BLOCK, width), jnp.bfloat16),
@@ -198,28 +207,21 @@
             vmem_limit_bytes=60 * 1024 * 1024, collective_id=0, has_side_effects=True
         ),
         cost_estimate=pl.CostEstimate(flops=flops, transcendentals=0, bytes_accessed=8 * 1024 * 1024),
-    )(coef, utaps, vtaps, level, trig, template, grid)
+    )(coef, utaps, vtaps, template, grid)
 
 
 def local(exposure, slots, target_rows, template, row_taps, col_taps, coef):
     e_rows, width = exposure.shape
     p_rows = template.shape[0]
     n_slots = 2 * SPAN + 1
-    slot_ids = slots[:, 0]
-    flat_place = slot_ids * p_rows + target_rows
-    select = (jnp.arange(n_slots * p_rows, dtype=jnp.int32)[:, None] == flat_place[None, :]).astype(jnp.float32)
+    place = jnp.arange(n_slots * p_rows, dtype=jnp.int32)
+    select = (
+        (place[:, None] // p_rows == slots[None, :, 0]) & (place[:, None] % p_rows == target_rows[None, :])
+    ).astype(jnp.float32)
     partial = jnp.dot(
         select, exposure, precision=lax.Precision.HIGHEST, preferred_element_type=jnp.float32
     ).reshape(n_slots, p_rows, width)
-    total_rows = p_rows * lax.axis_size("dec")
-    total_cols = width * lax.axis_size("ra")
-    rows_y = lax.axis_index("dec") * p_rows + jnp.arange(p_rows, dtype=jnp.int32)
-    level = (2 * rows_y + 1).astype(jnp.float32) / total_rows - 1.0
-    cols_x = lax.axis_index("ra") * width + jnp.arange(width, dtype=jnp.int32)
-    phase = (2 * cols_x + 1).astype(jnp.float32) * (math.pi / total_cols)
-    trig = jnp.stack([jnp.cos(phase), jnp.sin(phase)])
-
-    return difference_image(template, partial, row_taps, col_taps, coef, level, trig)
+    return difference_image(template, partial, row_taps, col_taps, coef)
 
 
 def solution(mesh):

time: 78.1 us -> 75.1 us (0.962)
  the two profiles are of different devices: /device:TPU:321 before, /device:TPU:383 now
where the time goes in v6:
time: 75.1 us; the launch traced here: 74.8 us
  Pallas kernels  65 us (87%)
  local copies, waits for them, and re-layouts  5 us (7%)
  matrix products  3.59 us (5%)
  other arithmetic  1.23 us (2%)
    pallas_call x1, Pallas kernels, difference_image(): pl.pallas_call(functools.partial(conv_kernel, n_tiles, n_basis, p_rows),...  65 us
    unnamed x6, local copies, waits for them, and re-layouts  5 us
    dot_general x1, matrix products, local(): jnp.dot(select, exposure, precision=lax.Precision.HIGHEST, preferred_elem...  3.59 us

profile of v6, /device:TPU:383, one launch (start us, length us, event | category | flops | bytes accessed | tf_op | source)
XLA Modules:
  0.0 74.8 jit_solution(18322126184692512117)
XLA Ops:
  0.0 0.0 copy-start
  0.0 0.9 %copy.8 = bf16[45,21]{1,0:T(8,128)(2,1)S(1)} copy(bf16[45,21]{0,1:T(8,128)(2,1)} %param.11) | data formatting | bytes 3780 | tf_op args[4]
  1.0 0.8 %copy.9 = bf16[45,21]{1,0:T(8,128)(2,1)S(1)} copy(bf16[45,21]{0,1:T(8,128)(2,1)} %param.12) | data formatting | bytes 3780 | tf_op args[5]
  1.8 0.6 pad_convert_fusion.1.vtaps_ref
  2.4 1.4 %copy.10.coef_ref = f32[45,6]{1,0:T(8,128)} copy(f32[45,6]{0,1:T(8,128)} %param.13) | data formatting | bytes 2160 | tf_op args[6]
  3.7 0.6 pad_convert_fusion.utaps_ref
  4.4 0.0 copy-done
  4.4 3.6 %fusion = f32[320,2048]{1,0:T(8,128)} fusion(f32[256,2048]{1,0:T(8,128)S(1)} %copy-done, s32[256]{0:T(256)} %param.9, s32[256]{0:T(256)} %bitcast.4, s32[320]{0:T(512)S(1)} %get-tuple-element.5, s32[320]{0:T(512)S(1)} %get-tuple-element.6), kind=kOutput, calls=%fused_computation | convolution fusion | flops 2013511680 | bytes 4723200 | tf_op jit(solution)/shard_map/dot_general | solution.py:221
  8.0 65.0 %shard_map.73 = f32[64,2048]{1,0:T(8,128)} custom-call(f32[45,6]{1,0:T(8,128)} %copy.10.coef_ref, f32[46,256]{1,0:T(8,128)} %pad_convert_fusion.utaps_ref, f32[46,128]{1,0:T(8,128)} %pad_convert_fusion.1.vtaps_ref, bf16[64,2048]{1,0:T(8,128)(2,1)} %template_ref.1, f32[5,64,2048]{2,1,0:T(8,128)} %bitcast.3), custom_call_target="tpu_custom_call" | custom-call | flops 13891534848 | bytes 8388608 | tf_op jit(solution)/shard_map/pallas_call | solution.py:189
  72.9 1.9 %copy.12 = f32[64,2048]{1,0:T(8,128)} copy(f32[64,2048]{1,0:T(8,128)} %shard_map.73) | data formatting | bytes 1048576
  (1 shorter events, 0.0 us)
Async XLA Ops:
  0.0 4.4 %copy-start = (f32[256,2048]{1,0:T(8,128)S(1)}, f32[256,2048]{1,0:T(8,128)}, u32[]{:S(2)}) copy-start(f32[256,2048]{1,0:T(8,128)} %param.7) | copy-start | bytes 6291460

commit v7 on v6

--- a/solution.py
+++ b/solution.py
@@ -84,6 +84,25 @@
         ((-1, 1), bottom, left, low_rows, slice(0, TILE)),
         ((1, 1), bottom, right, low_rows, high_cols),
     ]
+    sign = 2 * lax.rem(ra, 2) - 1
+
+    def grid_copy(src, slot, d_ra):
+        return pltpu.make_async_remote_copy(
+            src_ref=src,
+            dst_ref=arrived_ref.at[slot],
+            send_sem=grid_send.at[slot],
+            recv_sem=grid_recv.at[slot],
+            device_id=peer(d_ra, 0),
+            device_id_type=MESH,
+        )
+
+    to_partner = grid_copy(grid_ref.at[SPAN - sign], OWN, -sign)
+    to_combine = grid_copy(grid_ref.at[SPAN - 2 * sign], MIXED, -sign)
+    far = grid_copy(grid_ref.at[SPAN + 2 * sign], FAR, 2 * sign)
+    near = grid_copy(combined_ref, NEAR, sign)
+    for copy in (to_partner, to_combine, far):
+        copy.start()
+
     halo_copies = []
     for n, ((s_ra, s_dec), my_rows, my_cols, rows, cols) in enumerate(pieces):
         copy = pltpu.make_async_remote_copy(
@@ -96,24 +115,6 @@
         )
         copy.start()
         halo_copies.append(copy)
-    sign = 2 * lax.rem(ra, 2) - 1
-
-    def grid_copy(src, slot, d_ra):
-        return pltpu.make_async_remote_copy(
-            src_ref=src,
-            dst_ref=arrived_ref.at[slot],
-            send_sem=grid_send.at[slot],
-            recv_sem=grid_recv.at[slot],
-            device_id=peer(d_ra, 0),
-            device_id_type=MESH,
-        )
-
-    to_partner = grid_copy(grid_ref.at[SPAN - sign], OWN, -sign)
-    to_combine = grid_copy(grid_ref.at[SPAN - 2 * sign], MIXED, -sign)
-    far = grid_copy(grid_ref.at[SPAN + 2 * sign], FAR, 2 * sign)
-    near = grid_copy(combined_ref, NEAR, sign)
-    for copy in (to_partner, to_combine, far):
-        copy.start()
 
     to_combine.wait_recv()
     combined_ref[...] = grid_ref[SPAN + sign] + arrived_ref[MIXED]

time: 75.1 us -> 79.8 us (1.063)
  the two profiles are of different devices: /device:TPU:383 before, /device:TPU:1 now
where the time goes in v7:
time: 79.8 us; the launch traced here: 79.5 us
  Pallas kernels  69.7 us (87%)
  local copies, waits for them, and re-layouts  5 us (6%)
  matrix products  3.59 us (4%)
  other arithmetic  1.23 us (2%)
    pallas_call x1, Pallas kernels, difference_image(): pl.pallas_call(functools.partial(conv_kernel, n_tiles, n_basis, p_rows),...  69.7 us
    unnamed x6, local copies, waits for them, and re-layouts  5 us
    dot_general x1, matrix products, local(): jnp.dot(select, exposure, precision=lax.Precision.HIGHEST, preferred_elem...  3.59 us

profile of v7, /device:TPU:1, one launch (start us, length us, event | category | flops | bytes accessed | tf_op | source)
XLA Modules:
  0.0 79.5 jit_solution(13673876520208822312)
XLA Ops:
  0.0 0.0 copy-start
  0.0 0.9 %copy.8 = bf16[45,21]{1,0:T(8,128)(2,1)S(1)} copy(bf16[45,21]{0,1:T(8,128)(2,1)} %param.11) | data formatting | bytes 3780 | tf_op args[4]
  1.0 0.8 %copy.9 = bf16[45,21]{1,0:T(8,128)(2,1)S(1)} copy(bf16[45,21]{0,1:T(8,128)(2,1)} %param.12) | data formatting | bytes 3780 | tf_op args[5]
  1.8 0.6 pad_convert_fusion.1.vtaps_ref
  2.4 1.4 %copy.10.coef_ref = f32[45,6]{1,0:T(8,128)} copy(f32[45,6]{0,1:T(8,128)} %param.13) | data formatting | bytes 2160 | tf_op args[6]
  3.7 0.6 pad_convert_fusion.utaps_ref
  4.4 0.0 copy-done
  4.4 3.6 %fusion = f32[320,2048]{1,0:T(8,128)} fusion(f32[256,2048]{1,0:T(8,128)S(1)} %copy-done, s32[256]{0:T(256)} %param.9, s32[256]{0:T(256)} %bitcast.4, s32[320]{0:T(512)S(1)} %get-tuple-element.5, s32[320]{0:T(512)S(1)} %get-tuple-element.6), kind=kOutput, calls=%fused_computation | convolution fusion | flops 2013511680 | bytes 4723200 | tf_op jit(solution)/shard_map/dot_general | solution.py:222
  8.0 69.7 %shard_map.73 = f32[64,2048]{1,0:T(8,128)} custom-call(f32[45,6]{1,0:T(8,128)} %copy.10.coef_ref, f32[46,256]{1,0:T(8,128)} %pad_convert_fusion.utaps_ref, f32[46,128]{1,0:T(8,128)} %pad_convert_fusion.1.vtaps_ref, bf16[64,2048]{1,0:T(8,128)(2,1)} %template_ref.1, f32[5,64,2048]{2,1,0:T(8,128)} %bitcast.3), custom_call_target="tpu_custom_call" | custom-call | flops 13891534848 | bytes 8388608 | tf_op jit(solution)/shard_map/pallas_call | solution.py:190
  77.7 1.9 %copy.12 = f32[64,2048]{1,0:T(8,128)} copy(f32[64,2048]{1,0:T(8,128)} %shard_map.73) | data formatting | bytes 1048576
  (1 shorter events, 0.0 us)
Async XLA Ops:
  0.0 4.4 %copy-start = (f32[256,2048]{1,0:T(8,128)S(1)}, f32[256,2048]{1,0:T(8,128)}, u32[]{:S(2)}) copy-start(f32[256,2048]{1,0:T(8,128)} %param.7) | copy-start | bytes 6291460

commit v8 on v6

--- a/solution.py
+++ b/solution.py
@@ -98,20 +98,42 @@
         halo_copies.append(copy)
     sign = 2 * lax.rem(ra, 2) - 1
 
-    def grid_copy(src, slot, d_ra):
-        return pltpu.make_async_remote_copy(
-            src_ref=src,
-            dst_ref=arrived_ref.at[slot],
-            send_sem=grid_send.at[slot],
-            recv_sem=grid_recv.at[slot],
-            device_id=peer(d_ra, 0),
-            device_id_type=MESH,
-        )
-
-    to_partner = grid_copy(grid_ref.at[SPAN - sign], OWN, -sign)
-    to_combine = grid_copy(grid_ref.at[SPAN - 2 * sign], MIXED, -sign)
-    far = grid_copy(grid_ref.at[SPAN + 2 * sign], FAR, 2 * sign)
-    near = grid_copy(combined_ref, NEAR, sign)
+    half = p_rows // 2
+
+    class GridCopy:
+        def __init__(self, src, slot, d_ra):
+            self.parts = [
+                pltpu.make_async_remote_copy(
+                    src_ref=src.at[h * half:(h + 1) * half],
+                    dst_ref=arrived_ref.at[slot, h * half:(h + 1) * half],
+                    send_sem=grid_send.at[2 * slot + h],
+                    recv_sem=grid_recv.at[2 * slot + h],
+                    device_id=peer(d_ra, 0),
+                    device_id_type=MESH,
+                )
+                for h in range(2)
+            ]
+
+        def start(self):
+            for part in self.parts:
+                part.start()
+
+        def wait(self):
+            for part in self.parts:
+                part.wait()
+
+        def wait_recv(self):
+            for part in self.parts:
+                part.wait_recv()
+
+        def wait_send(self):
+            for part in self.parts:
+                part.wait_send()
+
+    to_partner = GridCopy(grid_ref.at[SPAN - sign], OWN, -sign)
+    to_combine = GridCopy(grid_ref.at[SPAN - 2 * sign], MIXED, -sign)
+    far = GridCopy(grid_ref.at[SPAN + 2 * sign], FAR, 2 * sign)
+    near = GridCopy(combined_ref, NEAR, sign)
     for copy in (to_partner, to_combine, far):
         copy.start()
 
@@ -200,8 +222,8 @@
             pltpu.VMEM((p_rows, width), jnp.float32),
             pltpu.SemaphoreType.DMA((8,)),
             pltpu.SemaphoreType.DMA((8,)),
-            pltpu.SemaphoreType.DMA((n_out,)),
-            pltpu.SemaphoreType.DMA((n_out,)),
+            pltpu.SemaphoreType.DMA((2 * n_out,)),
+            pltpu.SemaphoreType.DMA((2 * n_out,)),
         ],
         compiler_params=pltpu.CompilerParams(
             vmem_limit_bytes=60 * 1024 * 1024, collective_id=0, has_side_effects=True

time: 75.1 us -> 75.1 us (level)
  no operation moved by 1% of the time
where the time goes in v8:
time: 75.1 us; the launch traced here: 74.9 us
  Pallas kernels  65 us (87%)
  local copies, waits for them, and re-layouts  5 us (7%)
  matrix products  3.59 us (5%)
  other arithmetic  1.23 us (2%)
    pallas_call x1, Pallas kernels, difference_image(): pl.pallas_call(functools.partial(conv_kernel, n_tiles, n_basis, p_rows),...  65 us
    unnamed x6, local copies, waits for them, and re-layouts  5 us
    dot_general x1, matrix products, local(): jnp.dot(select, exposure, precision=lax.Precision.HIGHEST, preferred_elem...  3.59 us

profile of v8, /device:TPU:383, one launch (start us, length us, event | category | flops | bytes accessed | tf_op | source)
XLA Modules:
  0.0 74.9 jit_solution(3302410826592030837)
XLA Ops:
  0.0 0.0 copy-start
  0.0 0.9 %copy.8 = bf16[45,21]{1,0:T(8,128)(2,1)S(1)} copy(bf16[45,21]{0,1:T(8,128)(2,1)} %param.11) | data formatting | bytes 3780 | tf_op args[4]
  1.0 0.8 %copy.9 = bf16[45,21]{1,0:T(8,128)(2,1)S(1)} copy(bf16[45,21]{0,1:T(8,128)(2,1)} %param.12) | data formatting | bytes 3780 | tf_op args[5]
  1.8 0.6 pad_convert_fusion.1.vtaps_ref
  2.4 1.4 %copy.10.coef_ref = f32[45,6]{1,0:T(8,128)} copy(f32[45,6]{0,1:T(8,128)} %param.13) | data formatting | bytes 2160 | tf_op args[6]
  3.7 0.6 pad_convert_fusion.utaps_ref
  4.4 0.0 copy-done
  4.4 3.6 %fusion = f32[320,2048]{1,0:T(8,128)} fusion(f32[256,2048]{1,0:T(8,128)S(1)} %copy-done, s32[256]{0:T(256)} %param.9, s32[256]{0:T(256)} %bitcast.4, s32[320]{0:T(512)S(1)} %get-tuple-element.5, s32[320]{0:T(512)S(1)} %get-tuple-element.6), kind=kOutput, calls=%fused_computation | convolution fusion | flops 2013511680 | bytes 4723200 | tf_op jit(solution)/shard_map/dot_general | solution.py:243
  8.0 65.0 %shard_map.73 = f32[64,2048]{1,0:T(8,128)} custom-call(f32[45,6]{1,0:T(8,128)} %copy.10.coef_ref, f32[46,256]{1,0:T(8,128)} %pad_convert_fusion.utaps_ref, f32[46,128]{1,0:T(8,128)} %pad_convert_fusion.1.vtaps_ref, bf16[64,2048]{1,0:T(8,128)(2,1)} %template_ref.1, f32[5,64,2048]{2,1,0:T(8,128)} %bitcast.3), custom_call_target="tpu_custom_call" | custom-call | flops 13891534848 | bytes 8388608 | tf_op jit(solution)/shard_map/pallas_call | solution.py:211
  73.0 1.9 %copy.12 = f32[64,2048]{1,0:T(8,128)} copy(f32[64,2048]{1,0:T(8,128)} %shard_map.73) | data formatting | bytes 1048576
  (1 shorter events, 0.0 us)
Async XLA Ops:
  0.0 4.4 %copy-start = (f32[256,2048]{1,0:T(8,128)S(1)}, f32[256,2048]{1,0:T(8,128)}, u32[]{:S(2)}) copy-start(f32[256,2048]{1,0:T(8,128)} %param.7) | copy-start | bytes 6291460

commit v9 on v6

--- a/solution.py
+++ b/solution.py
@@ -49,8 +49,27 @@
         rp_ref[k * BLOCK + ROWS_PAD:(k + 1) * BLOCK, :] = jnp.zeros((BLOCK - ROWS_PAD, rp_ref.shape[1]), bf16)
 
 
+def presum_rows(exposure_ref, slot_ref, target_ref, grid_ref, p_rows):
+    f32, bf16 = jnp.float32, jnp.bfloat16
+    n_slots, e_rows = grid_ref.shape[0], exposure_ref.shape[0]
+    place = lax.broadcasted_iota(jnp.int32, (n_slots * p_rows, e_rows), 0)
+    select = ((place // p_rows == slot_ref[...]) & (place % p_rows == target_ref[...])).astype(bf16)
+    chunk = 512
+    for c in range(exposure_ref.shape[1] // chunk):
+        rows = exposure_ref[:, c * chunk:(c + 1) * chunk]
+        first = rows.astype(bf16)
+        rest = rows - first.astype(f32)
+        second = rest.astype(bf16)
+        third = (rest - second.astype(f32)).astype(bf16)
+        total = jnp.dot(select, first, preferred_element_type=f32)
+        total = total + jnp.dot(select, second, preferred_element_type=f32)
+        total = total + jnp.dot(select, third, preferred_element_type=f32)
+        for slot in range(n_slots):
+            grid_ref[slot, :, c * chunk:(c + 1) * chunk] = total[slot * p_rows:(slot + 1) * p_rows]
+
+
 def conv_kernel(n_tiles, n_basis, p_rows, coef_ref, utaps_ref, vtaps_ref, template_ref,
-                grid_ref, out_ref, rp_ref, windows_ref, weights_ref, ext_ref, arrived_ref, combined_ref,
+                exposure_ref, slot_ref, target_ref, out_ref, grid_ref, rp_ref, windows_ref, weights_ref, ext_ref, arrived_ref, combined_ref,
                 halo_send, halo_recv, grid_send, grid_recv):
     f32, bf16 = jnp.float32, jnp.bfloat16
     n_ra, n_dec = lax.axis_size("ra"), lax.axis_size("dec")
@@ -67,6 +86,7 @@
         pl.semaphore_signal(barrier, inc=1, device_id=peer(d_ra, d_dec), device_id_type=MESH)
 
     build_weights(coef_ref, vtaps_ref, weights_ref, rp_ref, n_basis, p_rows)
+    presum_rows(exposure_ref, slot_ref, target_ref, grid_ref, p_rows)
     pl.semaphore_wait(barrier, len(partners))
 
     top, bottom = slice(p_rows - EDGE, p_rows), slice(0, EDGE)
@@ -176,7 +196,7 @@
     out_ref[...] = science - out_ref[...]
 
 
-def difference_image(template, grid, row_taps, col_taps, coef):
+def difference_image(template, exposure, slot_row, target_row, row_taps, col_taps, coef):
     p_rows, width = template.shape
     n_tiles = width // TILE
     k_count = row_taps.shape[0]
@@ -189,9 +209,10 @@
     return pl.pallas_call(
         functools.partial(conv_kernel, n_tiles, n_basis, p_rows),
         out_shape=jax.ShapeDtypeStruct((p_rows, width), jnp.float32),
-        in_specs=[pl.BlockSpec(memory_space=pltpu.SMEM)] + [vmem] * 4,
+        in_specs=[pl.BlockSpec(memory_space=pltpu.SMEM)] + [vmem] * 6,
         out_specs=vmem,
         scratch_shapes=[
+            pltpu.VMEM((2 * SPAN + 1, p_rows, width), jnp.float32),
             pltpu.VMEM((n_basis * BLOCK, width), jnp.bfloat16),
             pltpu.VMEM((n_tiles * ROWS_PAD, WIN), jnp.bfloat16),
             pltpu.VMEM((6 * p_rows, n_basis * BLOCK), jnp.bfloat16),
@@ -207,21 +228,16 @@
             vmem_limit_bytes=60 * 1024 * 1024, collective_id=0, has_side_effects=True
         ),
         cost_estimate=pl.CostEstimate(flops=flops, transcendentals=0, bytes_accessed=8 * 1024 * 1024),
-    )(coef, utaps, vtaps, template, grid)
+    )(coef, utaps, vtaps, template, exposure, slot_row, target_row)
 
 
 def local(exposure, slots, target_rows, template, row_taps, col_taps, coef):
     e_rows, width = exposure.shape
     p_rows = template.shape[0]
     n_slots = 2 * SPAN + 1
-    place = jnp.arange(n_slots * p_rows, dtype=jnp.int32)
-    select = (
-        (place[:, None] // p_rows == slots[None, :, 0]) & (place[:, None] % p_rows == target_rows[None, :])
-    ).astype(jnp.float32)
-    partial = jnp.dot(
-        select, exposure, precision=lax.Precision.HIGHEST, preferred_element_type=jnp.float32
-    ).reshape(n_slots, p_rows, width)
-    return difference_image(template, partial, row_taps, col_taps, coef)
+    slot_row = slots.reshape(1, e_rows)
+    target_row = target_rows.reshape(1, e_rows)
+    return difference_image(template, exposure, slot_row, target_row, row_taps, col_taps, coef)
 
 
 def solution(mesh):

time: 75.1 us -> 73 us (0.972)
  the two profiles are of different devices: /device:TPU:383 before, /device:TPU:39 now
where the time goes in v9:
time: 73 us; the launch traced here: 72.7 us
  Pallas kernels  66.7 us (91%)
  local copies, waits for them, and re-layouts  4.84 us (7%)
  other arithmetic  1.24 us (2%)
    pallas_call x1, Pallas kernels, difference_image(): pl.pallas_call(functools.partial(conv_kernel, n_tiles, n_basis, p_rows),...  66.7 us
    unnamed x4, local copies, waits for them, and re-layouts  4.84 us

profile of v9, /device:TPU:39, one launch (start us, length us, event | category | flops | bytes accessed | tf_op | source)
XLA Modules:
  0.0 72.7 jit_solution(14276237509359323825)
XLA Ops:
  0.0 0.8 %copy.8 = bf16[45,21]{1,0:T(8,128)(2,1)S(1)} copy(bf16[45,21]{0,1:T(8,128)(2,1)} %param.11) | data formatting | bytes 3780 | tf_op args[4]
  0.8 0.8 %copy.9 = bf16[45,21]{1,0:T(8,128)(2,1)S(1)} copy(bf16[45,21]{0,1:T(8,128)(2,1)} %param.12) | data formatting | bytes 3780 | tf_op args[5]
  1.6 0.6 pad_convert_fusion.1.vtaps_ref
  2.2 1.4 %copy.10.coef_ref = f32[45,6]{1,0:T(8,128)} copy(f32[45,6]{0,1:T(8,128)} %param.13) | data formatting | bytes 2160 | tf_op args[6]
  3.6 0.6 pad_convert_fusion.utaps_ref
  4.2 66.7 %shard_map.73 = f32[64,2048]{1,0:T(8,128)} custom-call(f32[45,6]{1,0:T(8,128)} %copy.10.coef_ref, f32[46,256]{1,0:T(8,128)} %pad_convert_fusion.utaps_ref, f32[46,128]{1,0:T(8,128)} %pad_convert_fusion.1.vtaps_ref, bf16[64,2048]{1,0:T(8,128)(2,1)} %template_ref.1, f32[256,2048]{1,0:T(8,128)} %exposure_ref.1, s32[1,256]{1,0:T(1,128)} %bitcast.2, s32[1,256]{1,0:T(1,128)} %bitcast.3), custom_call_target="tpu_custom_call" | custom-call | flops 13891534848 | bytes 8388608 | tf_op jit(solution)/shard_map/pallas_call | solution.py:209
  70.9 1.9 %copy.12 = f32[64,2048]{1,0:T(8,128)} copy(f32[64,2048]{1,0:T(8,128)} %shard_map.73) | data formatting | bytes 1048576

commit v10 on v9

--- a/solution.py
+++ b/solution.py
@@ -85,7 +85,6 @@
     for d_ra, d_dec in partners:
         pl.semaphore_signal(barrier, inc=1, device_id=peer(d_ra, d_dec), device_id_type=MESH)
 
-    build_weights(coef_ref, vtaps_ref, weights_ref, rp_ref, n_basis, p_rows)
     presum_rows(exposure_ref, slot_ref, target_ref, grid_ref, p_rows)
     pl.semaphore_wait(barrier, len(partners))
 
@@ -138,6 +137,7 @@
     to_combine.wait_recv()
     combined_ref[...] = grid_ref[SPAN + sign] + arrived_ref[MIXED]
     near.start()
+    build_weights(coef_ref, vtaps_ref, weights_ref, rp_ref, n_basis, p_rows)
     for copy in halo_copies:
         copy.wait()
     keep_top = dec > 0

time: 73 us -> 72.6 us (level)
  the two profiles are of different devices: /device:TPU:39 before, /device:TPU:64 now
where the time goes in v10:
time: 72.6 us; the launch traced here: 72.3 us
  Pallas kernels  66.2 us (91%)
  local copies, waits for them, and re-layouts  4.84 us (7%)
  other arithmetic  1.24 us (2%)
    pallas_call x1, Pallas kernels, difference_image(): pl.pallas_call(functools.partial(conv_kernel, n_tiles, n_basis, p_rows),...  66.2 us
    unnamed x4, local copies, waits for them, and re-layouts  4.84 us

profile of v10, /device:TPU:64, one launch (start us, length us, event | category | flops | bytes accessed | tf_op | source)
XLA Modules:
  0.0 72.3 jit_solution(12806353856542877311)
XLA Ops:
  0.0 0.8 %copy.8 = bf16[45,21]{1,0:T(8,128)(2,1)S(1)} copy(bf16[45,21]{0,1:T(8,128)(2,1)} %param.11) | data formatting | bytes 3780 | tf_op args[4]
  0.8 0.8 %copy.9 = bf16[45,21]{1,0:T(8,128)(2,1)S(1)} copy(bf16[45,21]{0,1:T(8,128)(2,1)} %param.12) | data formatting | bytes 3780 | tf_op args[5]
  1.6 0.6 pad_convert_fusion.1.vtaps_ref
  2.2 1.4 %copy.10.coef_ref = f32[45,6]{1,0:T(8,128)} copy(f32[45,6]{0,1:T(8,128)} %param.13) | data formatting | bytes 2160 | tf_op args[6]
  3.6 0.6 pad_convert_fusion.utaps_ref
  4.2 66.2 %shard_map.73 = f32[64,2048]{1,0:T(8,128)} custom-call(f32[45,6]{1,0:T(8,128)} %copy.10.coef_ref, f32[46,256]{1,0:T(8,128)} %pad_convert_fusion.utaps_ref, f32[46,128]{1,0:T(8,128)} %pad_convert_fusion.1.vtaps_ref, bf16[64,2048]{1,0:T(8,128)(2,1)} %template_ref.1, f32[256,2048]{1,0:T(8,128)} %exposure_ref.1, s32[1,256]{1,0:T(1,128)} %bitcast.2, s32[1,256]{1,0:T(1,128)} %bitcast.3), custom_call_target="tpu_custom_call" | custom-call | flops 13891534848 | bytes 8388608 | tf_op jit(solution)/shard_map/pallas_call | solution.py:209
  70.5 1.9 %copy.12 = f32[64,2048]{1,0:T(8,128)} copy(f32[64,2048]{1,0:T(8,128)} %shard_map.73) | data formatting | bytes 1048576

commit v11 on v10

--- a/solution.py
+++ b/solution.py
@@ -70,6 +70,7 @@
 
 def conv_kernel(n_tiles, n_basis, p_rows, coef_ref, utaps_ref, vtaps_ref, template_ref,
                 exposure_ref, slot_ref, target_ref, out_ref, grid_ref, rp_ref, windows_ref, weights_ref, ext_ref, arrived_ref, combined_ref,
+                inner_ref, band_ref,
                 halo_send, halo_recv, grid_send, grid_recv):
     f32, bf16 = jnp.float32, jnp.bfloat16
     n_ra, n_dec = lax.axis_size("ra"), lax.axis_size("dec")
@@ -138,6 +139,33 @@
     combined_ref[...] = grid_ref[SPAN + sign] + arrived_ref[MIXED]
     near.start()
     build_weights(coef_ref, vtaps_ref, weights_ref, rp_ref, n_basis, p_rows)
+
+    inner = n_tiles - 2
+    for t in range(1, n_tiles - 1):
+        slab = template_ref[:, (t - 1) * TILE:(t + 2) * TILE].astype(f32)
+        slab = pltpu.roll(slab, 3 * TILE - (TILE - HALF), 1)
+        inner_ref[(t - 1) * p_rows:t * p_rows, :] = slab[:, 0:WIN].astype(bf16)
+
+    def inner_step(step, carry):
+        bands = []
+        for half in range(2):
+            urow = jnp.broadcast_to(utaps_ref[pl.ds(2 * step + half, 1), :], (TILE, WIN))
+            bands.append(pltpu.roll(urow, 0, 1, stride=1, stride_axis=0))
+        band_t = jnp.concatenate(bands, axis=0).astype(bf16)
+        band_ref[step] = band_t
+        part = lax.dot_general(
+            inner_ref[...], band_t, (((1,), (1,)), ((), ())), preferred_element_type=f32
+        ).astype(bf16)
+        for half in range(2):
+            base = pl.multiple_of((2 * step + half) * BLOCK + EDGE, EDGE)
+            for t in range(1, n_tiles - 1):
+                rp_ref[pl.ds(base, p_rows), t * TILE:(t + 1) * TILE] = part[
+                    (t - 1) * p_rows:t * p_rows, half * TILE:(half + 1) * TILE
+                ]
+        return carry
+
+    lax.fori_loop(0, n_basis // 2, inner_step, 0)
+
     for copy in halo_copies:
         copy.wait()
     keep_top = dec > 0
@@ -146,26 +174,30 @@
     ext_ref[EDGE + p_rows:, :] = jnp.where(
         keep_bottom, ext_ref[EDGE + p_rows:, :], jnp.zeros_like(ext_ref[EDGE + p_rows:, :])
     )
+    edge_rows = 2 * EDGE * n_tiles
     for t in range(n_tiles):
         slab = ext_ref[:, t * TILE:t * TILE + 3 * TILE].astype(f32)
-        slab = pltpu.roll(slab, 3 * TILE - (TILE - HALF), 1)
-        windows_ref[t * ROWS_PAD:(t + 1) * ROWS_PAD, :] = slab[:, 0:WIN].astype(bf16)
+        slab = pltpu.roll(slab, 3 * TILE - (TILE - HALF), 1)[:, 0:WIN].astype(bf16)
+        windows_ref[2 * EDGE * t:2 * EDGE * t + EDGE, :] = slab[0:EDGE]
+        windows_ref[2 * EDGE * t + EDGE:2 * EDGE * (t + 1), :] = slab[EDGE + p_rows:]
+        if t in (0, n_tiles - 1):
+            at = edge_rows + (0 if t == 0 else p_rows)
+            windows_ref[at:at + p_rows, :] = slab[EDGE:EDGE + p_rows]
 
     def row_step(step, carry):
-        bands = []
-        for half in range(2):
-            urow = jnp.broadcast_to(utaps_ref[pl.ds(2 * step + half, 1), :], (TILE, WIN))
-            bands.append(pltpu.roll(urow, 0, 1, stride=1, stride_axis=0))
-        band_t = jnp.concatenate(bands, axis=0).astype(bf16)
         part = lax.dot_general(
-            windows_ref[...], band_t, (((1,), (1,)), ((), ())), preferred_element_type=f32
+            windows_ref[...], band_ref[step], (((1,), (1,)), ((), ())), preferred_element_type=f32
         ).astype(bf16)
         for half in range(2):
             base = pl.multiple_of((2 * step + half) * BLOCK, BLOCK)
+            cols = slice(half * TILE, (half + 1) * TILE)
             for t in range(n_tiles):
-                rp_ref[pl.ds(base, ROWS_PAD), t * TILE:(t + 1) * TILE] = part[
-                    t * ROWS_PAD:(t + 1) * ROWS_PAD, half * TILE:(half + 1) * TILE
-                ]
+                tile = slice(t * TILE, (t + 1) * TILE)
+                rp_ref[pl.ds(base, EDGE), tile] = part[2 * EDGE * t:2 * EDGE * t + EDGE, cols]
+                rp_ref[pl.ds(base + EDGE + p_rows, EDGE), tile] = part[2 * EDGE * t + EDGE:2 * EDGE * (t + 1), cols]
+            for t in (0, n_tiles - 1):
+                at = edge_rows + (0 if t == 0 else p_rows)
+                rp_ref[pl.ds(base + EDGE, p_rows), t * TILE:(t + 1) * TILE] = part[at:at + p_rows, cols]
         return carry
 
     lax.fori_loop(0, n_basis // 2, row_step, 0)
@@ -214,11 +246,13 @@
         scratch_shapes=[
             pltpu.VMEM((2 * SPAN + 1, p_rows, width), jnp.float32),
             pltpu.VMEM((n_basis * BLOCK, width), jnp.bfloat16),
-            pltpu.VMEM((n_tiles * ROWS_PAD, WIN), jnp.bfloat16),
+            pltpu.VMEM((2 * EDGE * n_tiles + 2 * p_rows, WIN), jnp.bfloat16),
             pltpu.VMEM((6 * p_rows, n_basis * BLOCK), jnp.bfloat16),
             pltpu.VMEM((p_rows + 2 * EDGE, width + 2 * TILE), jnp.bfloat16),
             pltpu.VMEM((n_out, p_rows, width), jnp.float32),
             pltpu.VMEM((p_rows, width), jnp.float32),
+            pltpu.VMEM(((n_tiles - 2) * p_rows, WIN), jnp.bfloat16),
+            pltpu.VMEM((n_basis // 2, 2 * TILE, WIN), jnp.bfloat16),
             pltpu.SemaphoreType.DMA((8,)),
             pltpu.SemaphoreType.DMA((8,)),
             pltpu.SemaphoreType.DMA((n_out,)),

time: 72.6 us -> 67.2 us (0.926)
  Pallas kernels: 66.2 us -> 60.8 us
    pallas_call x1, Pallas kernels: 66.2 us -> 60.8 us  [difference_image(): pl.pallas_call(functools.partial(conv_kernel, n_tiles, n_basis, p_rows),...]
where the time goes in v11:
time: 67.2 us; the launch traced here: 66.9 us
  Pallas kernels  60.8 us (90%)
  local copies, waits for them, and re-layouts  4.84 us (7%)
  other arithmetic  1.24 us (2%)
    pallas_call x1, Pallas kernels, difference_image(): pl.pallas_call(functools.partial(conv_kernel, n_tiles, n_basis, p_rows),...  60.8 us
    unnamed x4, local copies, waits for them, and re-layouts  4.84 us

profile of v11, /device:TPU:64, one launch (start us, length us, event | category | flops | bytes accessed | tf_op | source)
XLA Modules:
  0.0 66.9 jit_solution(2914750698501069555)
XLA Ops:
  0.0 0.8 %copy.8 = bf16[45,21]{1,0:T(8,128)(2,1)S(1)} copy(bf16[45,21]{0,1:T(8,128)(2,1)} %param.11) | data formatting | bytes 3780 | tf_op args[4]
  0.8 0.8 %copy.9 = bf16[45,21]{1,0:T(8,128)(2,1)S(1)} copy(bf16[45,21]{0,1:T(8,128)(2,1)} %param.12) | data formatting | bytes 3780 | tf_op args[5]
  1.6 0.6 pad_convert_fusion.1.vtaps_ref
  2.2 1.4 %copy.10.coef_ref = f32[45,6]{1,0:T(8,128)} copy(f32[45,6]{0,1:T(8,128)} %param.13) | data formatting | bytes 2160 | tf_op args[6]
  3.6 0.6 pad_convert_fusion.utaps_ref
  4.2 60.8 %shard_map.73 = f32[64,2048]{1,0:T(8,128)} custom-call(f32[45,6]{1,0:T(8,128)} %copy.10.coef_ref, f32[46,256]{1,0:T(8,128)} %pad_convert_fusion.utaps_ref, f32[46,128]{1,0:T(8,128)} %pad_convert_fusion.1.vtaps_ref, bf16[64,2048]{1,0:T(8,128)(2,1)} %template_ref.1, f32[256,2048]{1,0:T(8,128)} %exposure_ref.1, s32[1,256]{1,0:T(1,128)} %bitcast.2, s32[1,256]{1,0:T(1,128)} %bitcast.3), custom_call_target="tpu_custom_call" | custom-call | flops 13891534848 | bytes 8388608 | tf_op jit(solution)/shard_map/pallas_call | solution.py:241
  65.0 1.9 %copy.12 = f32[64,2048]{1,0:T(8,128)} copy(f32[64,2048]{1,0:T(8,128)} %shard_map.73) | data formatting | bytes 1048576

commit v12 on v11

--- a/solution.py
+++ b/solution.py
@@ -175,14 +175,16 @@
         keep_bottom, ext_ref[EDGE + p_rows:, :], jnp.zeros_like(ext_ref[EDGE + p_rows:, :])
     )
     edge_rows = 2 * EDGE * n_tiles
+    shift = 3 * TILE - (TILE - HALF)
     for t in range(n_tiles):
-        slab = ext_ref[:, t * TILE:t * TILE + 3 * TILE].astype(f32)
-        slab = pltpu.roll(slab, 3 * TILE - (TILE - HALF), 1)[:, 0:WIN].astype(bf16)
-        windows_ref[2 * EDGE * t:2 * EDGE * t + EDGE, :] = slab[0:EDGE]
-        windows_ref[2 * EDGE * t + EDGE:2 * EDGE * (t + 1), :] = slab[EDGE + p_rows:]
+        cols = slice(t * TILE, t * TILE + 3 * TILE)
+        for rows, at in ((slice(0, EDGE), 2 * EDGE * t), (slice(EDGE + p_rows, 2 * EDGE + p_rows), 2 * EDGE * t + EDGE)):
+            slab = pltpu.roll(ext_ref[rows, cols].astype(f32), shift, 1)
+            windows_ref[at:at + EDGE, :] = slab[:, 0:WIN].astype(bf16)
         if t in (0, n_tiles - 1):
             at = edge_rows + (0 if t == 0 else p_rows)
-            windows_ref[at:at + p_rows, :] = slab[EDGE:EDGE + p_rows]
+            slab = pltpu.roll(ext_ref[EDGE:EDGE + p_rows, cols].astype(f32), shift, 1)
+            windows_ref[at:at + p_rows, :] = slab[:, 0:WIN].astype(bf16)
 
     def row_step(step, carry):
         part = lax.dot_general(

time: 67.2 us -> 67.2 us (level)
  no operation moved by 1% of the time
where the time goes in v12:
time: 67.2 us; the launch traced here: 66.9 us
  Pallas kernels  60.8 us (90%)
  local copies, waits for them, and re-layouts  4.84 us (7%)
  other arithmetic  1.24 us (2%)
    pallas_call x1, Pallas kernels, difference_image(): pl.pallas_call(functools.partial(conv_kernel, n_tiles, n_basis, p_rows),...  60.8 us
    unnamed x4, local copies, waits for them, and re-layouts  4.84 us

profile of v12, /device:TPU:64, one launch (start us, length us, event | category | flops | bytes accessed | tf_op | source)
XLA Modules:
  0.0 66.9 jit_solution(9616532879100256581)
XLA Ops:
  0.0 0.8 %copy.8 = bf16[45,21]{1,0:T(8,128)(2,1)S(1)} copy(bf16[45,21]{0,1:T(8,128)(2,1)} %param.11) | data formatting | bytes 3780 | tf_op args[4]
  0.8 0.8 %copy.9 = bf16[45,21]{1,0:T(8,128)(2,1)S(1)} copy(bf16[45,21]{0,1:T(8,128)(2,1)} %param.12) | data formatting | bytes 3780 | tf_op args[5]
  1.6 0.6 pad_convert_fusion.1.vtaps_ref
  2.2 1.4 %copy.10.coef_ref = f32[45,6]{1,0:T(8,128)} copy(f32[45,6]{0,1:T(8,128)} %param.13) | data formatting | bytes 2160 | tf_op args[6]
  3.6 0.6 pad_convert_fusion.utaps_ref
  4.2 60.8 %shard_map.73 = f32[64,2048]{1,0:T(8,128)} custom-call(f32[45,6]{1,0:T(8,128)} %copy.10.coef_ref, f32[46,256]{1,0:T(8,128)} %pad_convert_fusion.utaps_ref, f32[46,128]{1,0:T(8,128)} %pad_convert_fusion.1.vtaps_ref, bf16[64,2048]{1,0:T(8,128)(2,1)} %template_ref.1, f32[256,2048]{1,0:T(8,128)} %exposure_ref.1, s32[1,256]{1,0:T(1,128)} %bitcast.2, s32[1,256]{1,0:T(1,128)} %bitcast.3), custom_call_target="tpu_custom_call" | custom-call | flops 13891534848 | bytes 8388608 | tf_op jit(solution)/shard_map/pallas_call | solution.py:243
  65.0 1.9 %copy.12 = f32[64,2048]{1,0:T(8,128)} copy(f32[64,2048]{1,0:T(8,128)} %shard_map.73) | data formatting | bytes 1048576

commit v13 on v12

--- a/solution.py
+++ b/solution.py
@@ -204,7 +204,7 @@
 
     lax.fori_loop(0, n_basis // 2, row_step, 0)
 
-    chunk = 256
+    chunk = 512
 
     def col_step(step, carry):
         col = pl.multiple_of(step * chunk, chunk)

time: 67.2 us -> 66.4 us (0.988)
  Pallas kernels: 60.8 us -> 60 us
    pallas_call x1, Pallas kernels: 60.8 us -> 60 us  [difference_image(): pl.pallas_call(functools.partial(conv_kernel, n_tiles, n_basis, p_rows),...]
where the time goes in v13:
time: 66.4 us; the launch traced here: 66.1 us
  Pallas kernels  60 us (90%)
  local copies, waits for them, and re-layouts  4.84 us (7%)
  other arithmetic  1.24 us (2%)
    pallas_call x1, Pallas kernels, difference_image(): pl.pallas_call(functools.partial(conv_kernel, n_tiles, n_basis, p_rows),...  60 us
    unnamed x4, local copies, waits for them, and re-layouts  4.84 us

profile of v13, /device:TPU:64, one launch (start us, length us, event | category | flops | bytes accessed | tf_op | source)
XLA Modules:
  0.0 66.1 jit_solution(9329989103866512263)
XLA Ops:
  0.0 0.8 %copy.8 = bf16[45,21]{1,0:T(8,128)(2,1)S(1)} copy(bf16[45,21]{0,1:T(8,128)(2,1)} %param.11) | data formatting | bytes 3780 | tf_op args[4]
  0.8 0.8 %copy.9 = bf16[45,21]{1,0:T(8,128)(2,1)S(1)} copy(bf16[45,21]{0,1:T(8,128)(2,1)} %param.12) | data formatting | bytes 3780 | tf_op args[5]
  1.6 0.6 pad_convert_fusion.1.vtaps_ref
  2.2 1.4 %copy.10.coef_ref = f32[45,6]{1,0:T(8,128)} copy(f32[45,6]{0,1:T(8,128)} %param.13) | data formatting | bytes 2160 | tf_op args[6]
  3.6 0.6 pad_convert_fusion.utaps_ref
  4.2 60.0 %shard_map.73 = f32[64,2048]{1,0:T(8,128)} custom-call(f32[45,6]{1,0:T(8,128)} %copy.10.coef_ref, f32[46,256]{1,0:T(8,128)} %pad_convert_fusion.utaps_ref, f32[46,128]{1,0:T(8,128)} %pad_convert_fusion.1.vtaps_ref, bf16[64,2048]{1,0:T(8,128)(2,1)} %template_ref.1, f32[256,2048]{1,0:T(8,128)} %exposure_ref.1, s32[1,256]{1,0:T(1,128)} %bitcast.2, s32[1,256]{1,0:T(1,128)} %bitcast.3), custom_call_target="tpu_custom_call" | custom-call | flops 13891534848 | bytes 8388608 | tf_op jit(solution)/shard_map/pallas_call | solution.py:243
  64.2 1.9 %copy.12 = f32[64,2048]{1,0:T(8,128)} copy(f32[64,2048]{1,0:T(8,128)} %shard_map.73) | data formatting | bytes 1048576
